TPU v7x, 128 devices: a whole 4x4x4 slice. The times are simulated.
128 devices in a mesh: db: 16 (over z, y), rack: 8 (over x, core).
Axes of the slice: x: 4, y: 4, z: 4, core: 2. Of those that a mesh axis runs over, the one named last changes fastest.
Arguments:
- queries: bfloat16 [8192, 8192], P('db', 'rack'), may hold values from -10 to 10
- cotangent: bfloat16 [8192, 8192], P('db', 'rack'), may hold values from -6 to 6
- database: bfloat16 [512, 128, 896], P('db'), may hold values from -6 to 6
- w_key: bfloat16 [896, 8192], P(None, 'rack'), may hold values from -0.20044593 to 0.20044593
- w_value: bfloat16 [896, 8192], P(None, 'rack'), may hold values from -0.1875 to 0.1875
- neighbour_owner: int32 [128, 2], P('db'), may hold values from 0 to 15, all different within a row; in each aligned block of 8 rows (0 to 7, 8 to 15, ...) at most 3 rows name the same one
- neighbour_slot: int32 [128, 2], P('db'), may hold values from 0 to 31
Outputs:
- attended: bfloat16 [8192, 8192], P('db', 'rack')
- grad_queries: bfloat16 [8192, 8192], P('db', 'rack')
- grad_w_key: float32 [896, 8192], P(None, 'rack')
- grad_w_value: float32 [896, 8192], P(None, 'rack')
- grad_database: bfloat16 [512, 128, 896], P('db', 'rack')
Inputs may be any that keep to these rules, and one draw needn't show every extreme that they name: `neighbour_owner`: the 2 owners of one span differ. Among the spans of one db index, no owner is named by more than 3 spans, a bound that some block reaches.
All inputs are finite; a program needn't handle non-finite values.
Results may differ from a plain program's by a relative error of at most 0.02.
The roundings to bfloat16 on the way count: a program that leaves them out, or rounds other values in their place, can miss the bound.
Values may be sent and summed in bfloat16 or wider, within the bound.
A program may use at most 192 MiB of HBM per device.

v0:
```python
import jax
import jax.numpy as jnp
from jax import lax
from jax.sharding import PartitionSpec as P

HD = 128
SPAN = 64
CAP = 3


def local(queries, cotangent, database, w_key, w_value, neighbour_owner, neighbour_slot):
    peer_count = lax.axis_size("db")
    rack_count = lax.axis_size("rack")
    span_count = neighbour_owner.shape[0]
    nbr_count = neighbour_owner.shape[1]
    use_count = span_count * nbr_count
    local_rows = database.shape[0]
    panel_len = database.shape[1]
    enc_width = database.shape[2]
    part_rows = panel_len // rack_count
    capacity = CAP
    features = w_key.shape[1]
    head_count = features // HD
    owners = neighbour_owner.reshape(use_count)
    offsets = neighbour_slot.reshape(use_count)
    marked = (owners[:, None] == jnp.arange(peer_count, dtype=jnp.int32)[None, :]).astype(jnp.int32)
    before = jnp.cumsum(marked, axis=0) - marked
    ranked = jnp.sum(before * marked, axis=1)
    target = owners * capacity + ranked
    wanted = jnp.full((peer_count * capacity,), local_rows, jnp.int32).at[target].set(offsets)
    asked_rows = lax.all_to_all(
        wanted.reshape(peer_count, capacity), "db", split_axis=0, concat_axis=0, tiled=True
    )
    picked = jnp.minimum(asked_rows, local_rows - 1).reshape(peer_count * capacity)
    answer = jnp.take(database, picked, axis=0).reshape(peer_count, capacity, panel_len, enc_width)
    arrived = lax.all_to_all(answer, "db", split_axis=0, concat_axis=0, tiled=True)
    panels = jnp.take(arrived.reshape(peer_count * capacity, panel_len, enc_width), target, axis=0)
    piece_rows = panels.shape[1]
    flat_piece = panels.reshape(use_count * piece_rows, enc_width)
    key_piece = jnp.dot(flat_piece, w_key, preferred_element_type=jnp.float32).astype(jnp.bfloat16)
    value_piece = jnp.dot(flat_piece, w_value, preferred_element_type=jnp.float32).astype(
        jnp.bfloat16
    )
    panels, key_rows, value_rows = (
        panels,
        key_piece.reshape(use_count, piece_rows, features),
        value_piece.reshape(use_count, piece_rows, features),
    )
    key_count = nbr_count * panel_len
    query_heads = queries.reshape(span_count, SPAN, head_count, HD)
    grad_heads = cotangent.reshape(span_count, SPAN, head_count, HD)
    key_heads = key_rows.reshape(span_count, key_count, head_count, HD)
    value_heads = value_rows.reshape(span_count, key_count, head_count, HD)
    score_scale = HD ** (-0.5)
    scores = (
        jnp.einsum("cihd,cjhd->chij", query_heads, key_heads, preferred_element_type=jnp.float32)
        * score_scale
    )
    weights_full = jax.nn.softmax(scores, axis=-1)
    weights_half = weights_full.astype(jnp.bfloat16)
    attended = jnp.einsum(
        "chij,cjhd->cihd", weights_half, value_heads, preferred_element_type=jnp.float32
    )
    attended = attended.astype(jnp.bfloat16).reshape(span_count * SPAN, features)
    grad_prob = jnp.einsum(
        "cihd,cjhd->chij", grad_heads, value_heads, preferred_element_type=jnp.float32
    )
    grad_value = jnp.einsum(
        "chij,cihd->cjhd", weights_half, grad_heads, preferred_element_type=jnp.float32
    ).astype(jnp.bfloat16)
    row_delta = jnp.sum(weights_full * grad_prob, axis=-1, keepdims=True)
    grad_score = (weights_full * (grad_prob - row_delta) * score_scale).astype(jnp.bfloat16)
    grad_query = jnp.einsum(
        "chij,cjhd->cihd", grad_score, key_heads, preferred_element_type=jnp.float32
    )
    grad_query = grad_query.astype(jnp.bfloat16).reshape(span_count * SPAN, features)
    grad_key = jnp.einsum(
        "chij,cihd->cjhd", grad_score, query_heads, preferred_element_type=jnp.float32
    ).astype(jnp.bfloat16)
    flat_rows = panels.reshape(use_count * panel_len, enc_width)
    key_flat = grad_key.reshape(use_count * panel_len, features)
    value_flat = grad_value.reshape(use_count * panel_len, features)
    contract = (((0,), (0,)), ((), ()))
    term_key = lax.dot_general(flat_rows, key_flat, contract, preferred_element_type=jnp.float32)
    term_value = lax.dot_general(
        flat_rows, value_flat, contract, preferred_element_type=jnp.float32
    )
    grad_w_key, grad_w_value = (
        lax.psum(term_key.astype(jnp.bfloat16), "db").astype(jnp.float32),
        lax.psum(term_value.astype(jnp.bfloat16), "db").astype(jnp.float32),
    )
    key_uses = grad_key.reshape(use_count, panel_len, features)
    value_uses = grad_value.reshape(use_count, panel_len, features)
    total = jnp.einsum("upf,ef->pue", key_uses, w_key, preferred_element_type=jnp.float32)
    shares = lax.psum_scatter(
        (
            total
            + jnp.einsum("upf,ef->pue", value_uses, w_value, preferred_element_type=jnp.float32)
        ).astype(jnp.bfloat16),
        "rack",
        scatter_dimension=0,
        tiled=True,
    )
    sending = jnp.transpose(shares, (1, 0, 2))
    outgoing = (
        jnp.zeros((peer_count * capacity, part_rows, enc_width), jnp.bfloat16)
        .at[target]
        .set(sending)
    )
    returned = lax.all_to_all(
        outgoing.reshape(peer_count, capacity, part_rows, enc_width),
        "db",
        split_axis=0,
        concat_axis=0,
        tiled=True,
    )
    selector = (
        asked_rows.reshape(peer_count * capacity)[:, None]
        == jnp.arange(local_rows, dtype=jnp.int32)[None, :]
    ).astype(jnp.bfloat16)
    summed = jnp.einsum(
        "npw,nr->rpw",
        returned.reshape(peer_count * capacity, part_rows, enc_width),
        selector,
        preferred_element_type=jnp.float32,
    )
    grad_database = summed.astype(jnp.bfloat16)
    return (attended, grad_query, grad_w_key, grad_w_value, grad_database)


def solution(mesh):
    return jax.shard_map(
        local,
        mesh=mesh,
        in_specs=(
            P("db", "rack"),
            P("db", "rack"),
            P("db", None, None),
            P(None, "rack"),
            P(None, "rack"),
            P("db", None),
            P("db", None),
        ),
        out_specs=(
            P("db", "rack"),
            P("db", "rack"),
            P(None, "rack"),
            P(None, "rack"),
            P("db", "rack", None),
        ),
        check_vma=False,
    )
```

profile of v0, /device:TPU:0, one launch (start us, length us, event | category | flops | bytes accessed | tf_op | source)
XLA Modules:
  0.0 473.9 jit_solution(6054036773196922508)
XLA Ops:
  11.7 15.5 %all_to_all.22 = s32[16,1,3]{2,1,0:T(1,128)S(1)} all-to-all(s32[16,1,3]{2,1,0:T(1,128)S(1)} %bitcast.164), channel_id=1, replica_groups=mesh['db'=16,'rack'=8] {'db'}, dimensions={0} | all-to-all | bytes 384 | tf_op jit(solution)/shard_map/all_to_all | solution.py:31
  28.7 9.9 %gather_fusion = bf16[48,128,896]{2,1,0:T(8,128)(2,1)} fusion(bf16[32,128,896]{2,1,0:T(8,128)(2,1)} %param.9, s32[1024]{0:T(1024)S(1)} %pad_clamp_fusion.1), kind=kCustom, calls=%fused_computation | custom fusion | bytes 22020288 | tf_op jit(solution)/shard_map/jit(_take)/gather | solution.py:35
  38.6 9.9 %broadcast_select_fusion = bf16[16,3,128,896]{3,2,1,0:T(8,128)(2,1)} fusion(bf16[16,3,128,896]{3,2,1,0:T(8,128)(2,1)} %bitcast.145, pred[16,3]{1,0:T(8,128)(4,1)S(1)} %copy.52), kind=kLoop, calls=%fused_computation.6 | loop fusion | flops 5505024 | bytes 22020144 | tf_op jit(solution)/shard_map/jit(_take)/select_n | solution.py:35
  48.5 5.0 %all-to-all-start.1 = ((bf16[16,3,128,896]{3,2,1,0:T(8,128)(2,1)}), bf16[16,3,128,896]{3,2,1,0:T(8,128)(2,1)}, u32[]{:S(2)}, u32[]{:S(2)}) async-start(bf16[16,3,128,896]{3,2,1,0:T(8,128)(2,1)} %broadcast_select_fusion), calls=%async_computation.1 | async-start | bytes 22020096 | tf_op jit(solution)/shard_map/all_to_all | solution.py:36
  56.4 156.4 %all-to-all-done.1 = bf16[16,3,128,896]{3,2,1,0:T(8,128)(2,1)} async-done(((bf16[16,3,128,896]{3,2,1,0:T(8,128)(2,1)}), bf16[16,3,128,896]{3,2,1,0:T(8,128)(2,1)}, u32[]{:S(2)}, u32[]{:S(2)}) %all-to-all-start.1) | async-done | bytes 11010080 | tf_op jit(solution)/shard_map/all_to_all | solution.py:36
  212.8 6.9 %gather_fusion.1 = bf16[16,128,896]{2,1,0:T(8,128)(2,1)} fusion(bf16[48,128,896]{2,1,0:T(8,128)(2,1)} %bitcast.7, s32[1024]{0:T(1024)S(1)} %pad_clamp_fusion), kind=kCustom, calls=%fused_computation.1 | custom fusion | bytes 7340096 | tf_op jit(solution)/shard_map/jit(_take)/gather | solution.py:37
  222.1 4.7 convert_bitcast_fusion.2
  228.3 5.1 %convert_bitcast_fusion.3 = bf16[256,8,8,128]{3,1,2,0:T(8,128)(2,1)S(1)} fusion(bf16[2048,896]{1,0:T(8,128)(2,1)S(1)} %bitcast_select_fusion, bf16[896,1024]{1,0:T(8,128)(2,1)S(1)} %copy-done.11), kind=kOutput, calls=%fused_computation.26 | convolution fusion | flops 3760193536 | bytes 9699328 | tf_op jit(solution)/shard_map/dot_general | solution.py:41
  243.1 14.3 %convert_bitcast_fusion = bf16[8,256,8,128]{3,1,2,0:T(8,128)(2,1)} fusion(bf16[8,64,8,128]{3,2,1,0:T(8,128)(2,1)} %bitcast.155, f32[8,8,64]{2,1,0:T(8,128)S(1)} %get-tuple-element.25, f32[8,8,256,64]{2,3,1,0:T(8,128)} %copy-done.3), kind=kOutput, calls=%fused_computation.23 | convolution fusion | flops 275779840 | bytes 9453568 | tf_op jit(solution)/shard_map/chij,cihd->cjhd/dot_general | solution.py:68
  257.3 31.9 %convert_bitcast_fusion.1 = bf16[8,256,8,128]{3,1,2,0:T(8,128)(2,1)} fusion(f32[8,8,256,64]{2,3,1,0:T(8,128)} %fusion.13, bf16[8,64,8,128]{3,2,1,0:T(8,128)(2,1)S(1)} %bitcast.154, f32[8,8,64,256]{3,2,1,0:T(8,128)} %get-tuple-element.26, f32[8,8,64]{2,1,0:T(8,128)S(1)} %get-tuple-element.25), kind=kOutput, calls=%fused_computation.24 | convolution fusion | flops 277876992 | bytes 13647872 | tf_op jit(solution)/shard_map/chij,cihd->cjhd/dot_general | solution.py:77
  289.3 7.1 %copy.62 = bf16[8,256,8,128]{3,2,1,0:T(8,128)(2,1)} copy(bf16[8,256,8,128]{3,1,2,0:T(8,128)(2,1)} %convert_bitcast_fusion.1) | data formatting | bytes 8388608 | tf_op jit(solution)/shard_map/convert_element_type | solution.py:79
  296.4 4.8 %copy.64 = bf16[8,256,8,128]{3,2,1,0:T(8,128)(2,1)} copy(bf16[8,256,8,128]{3,1,2,0:T(8,128)(2,1)S(1)} %copy-done.8) | data formatting | bytes 8388608 | tf_op jit(solution)/shard_map/convert_element_type | solution.py:70
  301.2 7.3 %reshape.196 = bf16[16,128,1024]{2,1,0:T(8,128)(2,1)} reshape(bf16[8,256,8,128]{3,2,1,0:T(8,128)(2,1)} %copy.62) | data formatting | bytes 8388608 | tf_op jit(solution)/shard_map/reshape | solution.py:92
  308.5 8.7 %fusion.28 = f32[16,128,896]{2,1,0:T(8,128)} fusion(bf16[16,128,1024]{2,1,0:T(8,128)(2,1)} %reshape.196, bf16[896,1024]{1,0:T(8,128)(2,1)S(1)} %copy-done), kind=kOutput, calls=%fused_computation.43 | convolution fusion | flops 3758096384 | bytes 13369344 | tf_op jit(solution)/shard_map/upf,ef->pue/dot_general | solution.py:94
  317.2 7.4 %reshape.197 = bf16[16,128,1024]{2,1,0:T(8,128)(2,1)} reshape(bf16[8,256,8,128]{3,2,1,0:T(8,128)(2,1)} %copy.64) | data formatting | bytes 8388608 | tf_op jit(solution)/shard_map/reshape | solution.py:93
  324.7 9.4 %fusion.22 = bf16[128,16,896]{2,0,1:T(8,128)(2,1)} fusion(f32[16,128,896]{2,1,0:T(8,128)} %fusion.28, bf16[16,128,1024]{2,1,0:T(8,128)(2,1)} %reshape.197, bf16[896,1024]{1,0:T(8,128)(2,1)S(1)} %copy-done.12), kind=kOutput, calls=%fused_computation.36 | convolution fusion | flops 3761766400 | bytes 17039360 | tf_op jit(solution)/shard_map/upf,ef->pue/dot_general | solution.py:98
  337.5 5.2 %fusion.30 = bf16[896,1024]{1,0:T(8,128)(2,1)} fusion(bf16[2048,896]{1,0:T(8,128)(2,1)S(1)} %bitcast.159, bf16[256,8,8,128]{3,2,1,0:T(8,128)(2,1)S(1)} %bitcast.150), kind=kOutput, calls=%fused_computation.45 | convolution fusion | flops 3759013888 | bytes 9699328 | tf_op jit(solution)/shard_map/dot_general | solution.py:84
  342.7 5.2 %fusion.33 = bf16[896,1024]{1,0:T(8,128)(2,1)} fusion(bf16[2048,896]{1,0:T(8,128)(2,1)S(1)} %bitcast.160, bf16[256,8,8,128]{3,2,1,0:T(8,128)(2,1)S(1)} %bitcast.151), kind=kOutput, calls=%fused_computation.46 | convolution fusion | flops 3759013888 | bytes 9699328 | tf_op jit(solution)/shard_map/dot_general | solution.py:85
  347.9 24.1 %reduce-scatter.2.cloned.1.call-done = bf16[16,16,896]{2,0,1:T(8,128)(2,1)} async-done(((bf16[128,16,896]{2,0,1:T(8,128)(2,1)}), bf16[16,16,896]{2,0,1:T(8,128)(2,1)}) %reduce-scatter.2.cloned.1.call-update) | async-done | bytes 458768 | tf_op jit(solution)/shard_map/reduce_scatter | solution.py:95
  376.1 7.4 %all-to-all-start.2 = ((bf16[16,3,16,896]{3,2,1,0:T(8,128)(2,1)}), bf16[16,3,16,896]{3,2,1,0:T(8,128)(2,1)S(1)}, u32[]{:S(2)}, u32[]{:S(2)}) async-start(bf16[16,3,16,896]{3,2,1,0:T(8,128)(2,1)} %bitcast.21), calls=%async_computation.3 | async-start | bytes 2752512 | tf_op jit(solution)/shard_map/all_to_all | solution.py:110
  383.6 29.5 %fusion.46 = bf16[8,64,8,128]{3,1,2,0:T(8,128)(2,1)} fusion(bf16[8,256,8,128]{3,2,1,0:T(8,128)(2,1)} %bitcast.149, f32[8,8,256,64]{2,3,1,0:T(8,128)} %fusion.13, f32[8,8,64,256]{3,2,1,0:T(8,128)} %get-tuple-element.26, f32[8,8,64]{2,1,0:T(8,128)S(1)} %get-tuple-element.25), kind=kOutput, calls=%fused_computation.52 | convolution fusion | flops 276304128 | bytes 13647872 | tf_op jit(solution)/shard_map/chij,cjhd->cihd/dot_general | solution.py:73
  415.0 13.1 %fusion.43 = bf16[8,64,8,128]{3,1,2,0:T(8,128)(2,1)} fusion(bf16[8,256,8,128]{3,2,1,0:T(8,128)(2,1)} %bitcast.147, f32[8,8,64]{2,1,0:T(8,128)S(1)} %get-tuple-element.25, f32[8,8,256,64]{2,3,1,0:T(8,128)} %copy-done.3), kind=kOutput, calls=%fused_computation.51 | convolution fusion | flops 274206976 | bytes 9453568 | tf_op jit(solution)/shard_map/chij,cjhd->cihd/dot_general | solution.py:61
  431.9 26.4 %all-reduce.3.cloned.1.call-done = (bf16[896,1024]{1,0:T(8,128)(2,1)}, bf16[896,1024]{1,0:T(8,128)(2,1)}) async-done(((bf16[896,1024]{1,0:T(8,128)(2,1)}, bf16[896,1024]{1,0:T(8,128)(2,1)}), (bf16[896,1024]{1,0:T(8,128)(2,1)}, bf16[896,1024]{1,0:T(8,128)(2,1)})) %all-reduce.3.cloned.1.call-update) | async-done | bytes 3670032 | tf_op jit(solution)/shard_map/psum | solution.py:89
  458.3 3.9 convert_element_type.73
  (73 shorter events, 38.5 us)
Async XLA Ops:
  8.0 214.1 %copy-start = (bf16[896,1024]{1,0:T(8,128)(2,1)S(1)}, bf16[896,1024]{1,0:T(8,128)(2,1)}, u32[]{:S(2)}) copy-start(bf16[896,1024]{1,0:T(8,128)(2,1)} %param.10) | copy-start | bytes 5505028
  48.5 5.1 %copy-start.10 = (bf16[512,1024]{1,0:T(8,128)(2,1)S(1)}, bf16[512,1024]{1,0:T(8,128)(2,1)}, u32[]{:S(2)}) copy-start(bf16[512,1024]{1,0:T(8,128)(2,1)} %param.8) | copy-start | bytes 3145732
  48.5 164.3 %all-to-all-start.1 = ((bf16[16,3,128,896]{3,2,1,0:T(8,128)(2,1)}), bf16[16,3,128,896]{3,2,1,0:T(8,128)(2,1)}, u32[]{:S(2)}, u32[]{:S(2)}) async-start(bf16[16,3,128,896]{3,2,1,0:T(8,128)(2,1)} %broadcast_select_fusion), calls=%async_computation.1 | async-start | bytes 22020096 | tf_op jit(solution)/shard_map/all_to_all | solution.py:36
  53.5 318.5 %reduce-scatter.2.cloned.1.call-start = ((), (), s32[]{:S(2)}) async-start(), calls=%async_computation.4 | async-start | bytes 4128768 | tf_op jit(solution)/shard_map/reduce_scatter | solution.py:95
  226.8 1.5 copy-start.11
  228.3 6.3 %copy-start.4 = (bf16[256,8,8,128]{3,2,1,0:T(8,128)(2,1)}, bf16[256,8,8,128]{3,2,1,0:T(8,128)(2,1)S(1)}, u32[]{:S(2)}) copy-start(bf16[256,8,8,128]{3,2,1,0:T(8,128)(2,1)S(1)} %copy.69) | copy-start | bytes 12582916
  234.6 4.9 %copy-start.2 = (bf16[256,8,8,128]{3,2,1,0:T(8,128)(2,1)}, bf16[256,8,8,128]{3,2,1,0:T(8,128)(2,1)S(1)}, u32[]{:S(2)}) copy-start(bf16[256,8,8,128]{3,2,1,0:T(8,128)(2,1)S(1)} %copy.71) | copy-start | bytes 12582916
  236.2 3.3 copy-start.3
  236.2 3.3 copy-start.7
  289.3 7.1 %copy-start.8 = (bf16[8,256,8,128]{3,1,2,0:T(8,128)(2,1)S(1)}, bf16[8,256,8,128]{3,1,2,0:T(8,128)(2,1)}, u32[]{:S(2)}) copy-start(bf16[8,256,8,128]{3,1,2,0:T(8,128)(2,1)} %convert_bitcast_fusion) | copy-start | bytes 12582916
  317.2 7.4 %copy-start.12 = (bf16[896,1024]{1,0:T(8,128)(2,1)S(1)}, bf16[896,1024]{1,0:T(8,128)(2,1)}, u32[]{:S(2)}) copy-start(bf16[896,1024]{1,0:T(8,128)(2,1)} %param.11) | copy-start | bytes 5505028
  334.1 124.2 %all-reduce.3.cloned.1.call-start = ((), (), s32[]{:S(2)}) async-start(), calls=%async_computation.5 | async-start | bytes 7340032 | tf_op jit(solution)/shard_map/psum | solution.py:89
  334.2 3.3 copy-start.5
  337.5 5.2 %copy-start.6 = (bf16[8,256,8,128]{3,2,1,0:T(8,128)(2,1)S(1)}, bf16[8,256,8,128]{3,2,1,0:T(8,128)(2,1)}, u32[]{:S(2)}) copy-start(bf16[8,256,8,128]{3,2,1,0:T(8,128)(2,1)} %copy.64) | copy-start | bytes 12582916
  376.1 88.4 %all-to-all-start.2 = ((bf16[16,3,16,896]{3,2,1,0:T(8,128)(2,1)}), bf16[16,3,16,896]{3,2,1,0:T(8,128)(2,1)S(1)}, u32[]{:S(2)}, u32[]{:S(2)}) async-start(bf16[16,3,16,896]{3,2,1,0:T(8,128)(2,1)} %bitcast.21), calls=%async_computation.3 | async-start | bytes 2752512 | tf_op jit(solution)/shard_map/all_to_all | solution.py:110
  458.3 3.9 copy-start.9
  462.2 3.9 copy-start.1
Sparse Core Ops, SparseCore 0:
  334.3 37.6 reduce-scatter.1
Sparse Core Ops, SparseCore 1:
  348.0 110.3 all-reduce.2
where the time goes:
time: 481 us; the launch traced here: 474 us
  waiting for transfers between devices  207 us (43%)
  matrix products  133 us (28%)
  local copies, waits for them, and re-layouts  64.3 us (13%)
  other arithmetic  25.8 us (5%)
  between operations  16.1 us (3%)
  blocking collectives  15.5 us (3%)
  starting transfers between devices  12.5 us (3%)
    all_to_all x1, waiting for transfers between devices, local(): lax.all_to_all(answer, 'db', split_axis=0, concat_axis=0, tiled=True)  156 us
    dot_general x1, matrix products, local(): jnp.einsum('chij,cihd->cjhd', grad_score, query_heads, preferred_element_...  31.9 us
    dot_general x1, matrix products, local(): jnp.einsum('chij,cjhd->cihd', grad_score, key_heads, preferred_element_ty...  29.5 us
    psum x1, waiting for transfers between devices, local(): lax.psum(term_key.astype(jnp.bfloat16), 'db').astype(jnp.float32)  26.4 us
    reduce_scatter x1, waiting for transfers between devices, local(): lax.psum_scatter((total + jnp.einsum('upf,ef->pue', value_uses, w_value,...  24.1 us
    all_to_all x1, blocking collectives, local(): lax.all_to_all(wanted.reshape(peer_count, capacity), 'db', split_axis=0,...  15.5 us
    dot_general x1, matrix products, local(): jnp.einsum('chij,cihd->cjhd', weights_half, grad_heads, preferred_element...  14.3 us
    dot_general x1, matrix products, local(): jnp.einsum('chij,cjhd->cihd', weights_half, value_heads, preferred_elemen...  13.1 us
  transfers between devices with their start and end apart: 4, of which 3 were waited for; matrix products, arithmetic and copies ran while one was open for 16% of the time, Pallas kernels for 0%

commit v1 on v0

v1 whole, which is shorter than its diff:
```python
import functools

import jax
import jax.numpy as jnp
from jax import lax
from jax.experimental import pallas as pl
from jax.experimental.pallas import tpu as pltpu
from jax.sharding import PartitionSpec as P

HD = 128
SPAN = 64
CAP = 3
NT = (((1,), (1,)), ((), ()))
TN = (((0,), (0,)), ((), ()))
F32 = jnp.float32
BF16 = jnp.bfloat16


def dot(a, b):
    return jnp.dot(a, b, preferred_element_type=F32)


def block_kernel(spans, heads, panels, queries, cotangent, w_key, w_value, attended, grad_queries, part_key, part_value,
                 use_grad, flipped, rows_kv, grads_kv):
    step = pl.program_id(0)
    keys = panels.shape[0] // spans
    width = panels.shape[1]
    scale = HD ** -0.5

    @pl.when(step == 0)
    def _():
        for c in range(spans):
            flipped[:, c * keys:(c + 1) * keys] = panels[c * keys:(c + 1) * keys, :].T

    @pl.when(step < heads)
    def _():
        columns = pl.ds(pl.multiple_of(step * HD, HD), HD)
        weights = jnp.concatenate([w_key[:, columns], w_value[:, columns]], axis=1)
        half = spans // 2 * keys
        for part in range(2):
            rows_kv[part * half:(part + 1) * half, :] = dot(panels[part * half:(part + 1) * half, :], weights).astype(BF16)
        zero = jnp.zeros((SPAN, HD), BF16)
        for c in range(spans):
            tokens = slice(c * SPAN, (c + 1) * SPAN)
            own = slice(c * keys, (c + 1) * keys)
            query, grad = queries[tokens, :], cotangent[tokens, :]
            both = rows_kv[own, :]
            left = jnp.concatenate(
                [jnp.concatenate([query, zero], axis=1), jnp.concatenate([zero, grad], axis=1)], axis=0
            )
            pair = lax.dot_general(left, both, NT, preferred_element_type=F32)
            scores, grad_probs = pair[:SPAN] * scale, pair[SPAN:]
            raised = jnp.exp(scores - jnp.max(scores, axis=-1, keepdims=True))
            probs = raised / jnp.sum(raised, axis=-1, keepdims=True)
            delta = jnp.sum(probs * grad_probs, axis=-1, keepdims=True)
            grad_scores = (probs * (grad_probs - delta) * scale).astype(BF16)
            stacked = jnp.concatenate([probs.astype(BF16), grad_scores], axis=0)
            out = dot(stacked, both)
            attended[tokens, :] = out[:SPAN, HD:].astype(BF16)
            grad_queries[tokens, :] = out[SPAN:, :HD].astype(BF16)
            right = jnp.concatenate(
                [jnp.concatenate([zero, grad], axis=1), jnp.concatenate([query, zero], axis=1)], axis=0
            )
            grads_kv[step, own, :] = lax.dot_general(stacked, right, TN, preferred_element_type=F32).astype(BF16)
        total = dot(flipped[...], grads_kv[step]).astype(BF16)
        part_key[...] = total[:, :HD]
        part_value[...] = total[:, HD:]

    @pl.when(step >= heads)
    def _():
        c = step - heads
        own = pl.ds(pl.multiple_of(c * keys, keys), keys)
        total = jnp.zeros((keys, width), F32)
        for h in range(heads):
            columns = slice(h * HD, (h + 1) * HD)
            weights = jnp.concatenate([w_key[:, columns], w_value[:, columns]], axis=1)
            total = total + lax.dot_general(grads_kv[h, own, :], weights, NT, preferred_element_type=F32)
        total = total.astype(BF16)
        pieces, uses, rows = use_grad.shape[0], use_grad.shape[1], use_grad.shape[2]
        for n in range(uses):
            for r in range(pieces):
                first = (n * pieces + r) * rows
                use_grad[r, n, :, :] = total[first:first + rows, :]


def block_call(panels, queries, cotangent, w_key, w_value, racks):
    uses, panel_len, width = panels.shape
    spans = queries.shape[0] // SPAN
    features = w_key.shape[1]
    heads = features // HD
    per_span = uses // spans
    rows = panel_len // racks
    total = uses * panel_len
    once = dict(pipeline_mode=pl.Buffered(1))
    by_head = lambda size: pl.BlockSpec((size, HD), lambda i: (0, jnp.minimum(i, heads - 1)))
    whole = lambda a, b: pl.BlockSpec((a, b), lambda i: (0, 0), **once)

    return pl.pallas_call(
        functools.partial(block_kernel, spans, heads),
        grid=(heads + spans,),
        out_shape=(
            jax.ShapeDtypeStruct(queries.shape, BF16),
            jax.ShapeDtypeStruct(queries.shape, BF16),
            jax.ShapeDtypeStruct((width, features), BF16),
            jax.ShapeDtypeStruct((width, features), BF16),
            jax.ShapeDtypeStruct((racks, uses, rows, width), BF16),
        ),
        in_specs=[
            whole(total, width), by_head(queries.shape[0]), by_head(queries.shape[0]), whole(width, features), whole(width, features),
        ],
        out_specs=[
            by_head(queries.shape[0]), by_head(queries.shape[0]), by_head(width), by_head(width),
            pl.BlockSpec((racks, per_span, rows, width), lambda i: (0, jnp.maximum(i - heads, 0), 0, 0)),
        ],
        scratch_shapes=[
            pltpu.VMEM((width, total), BF16),
            pltpu.VMEM((total, 2 * HD), BF16),
            pltpu.VMEM((heads, total, 2 * HD), BF16),
        ],
        compiler_params=pltpu.CompilerParams(vmem_limit_bytes=56 * 1024 * 1024),
        cost_estimate=pl.CostEstimate(flops=6 * total * width * features * 2, bytes_accessed=24 << 20, transcendentals=1 << 20),
        name="block",
    )(panels.reshape(total, width), queries, cotangent, w_key, w_value)


def pick(selector, source):
    return jnp.einsum("ns,spw->npw", selector, source, preferred_element_type=F32).astype(BF16)


def local(queries, cotangent, database, w_key, w_value, neighbour_owner, neighbour_slot):
    peer_count = lax.axis_size("db")
    racks = lax.axis_size("rack")
    span_count, nbr_count = neighbour_owner.shape
    use_count = span_count * nbr_count
    local_rows, panel_len, width = database.shape
    rows = panel_len // racks
    owners = neighbour_owner.reshape(use_count)
    offsets = neighbour_slot.reshape(use_count)
    earlier = jnp.arange(use_count)[None, :] < jnp.arange(use_count)[:, None]
    ranked = jnp.sum(((owners[:, None] == owners[None, :]) & earlier).astype(jnp.int32), axis=1)
    target = owners * CAP + ranked
    named = (target[None, :] == jnp.arange(peer_count * CAP, dtype=jnp.int32)[:, None]).astype(jnp.int32)
    wanted = jnp.sum(named * (offsets - local_rows)[None, :], axis=1) + local_rows
    asked_rows = lax.all_to_all(wanted.reshape(peer_count, CAP), "db", split_axis=0, concat_axis=0, tiled=True)
    own = lax.dynamic_slice_in_dim(database, lax.axis_index("rack") * rows, rows, 1)
    selector = (
        asked_rows.reshape(peer_count * CAP)[:, None] == jnp.arange(local_rows, dtype=jnp.int32)[None, :]
    ).astype(BF16)
    answer = pick(selector, own).reshape(peer_count, CAP, rows, width)
    arrived = lax.all_to_all(answer, "db", split_axis=0, concat_axis=0, tiled=True)
    placed = (target[:, None] == jnp.arange(peer_count * CAP, dtype=jnp.int32)[None, :]).astype(BF16)
    mine = pick(placed, arrived.reshape(peer_count * CAP, rows, width))
    panels = lax.all_gather(mine, "rack", axis=1, tiled=True)
    attended, grad_query, part_key, part_value, use_grad = block_call(panels, queries, cotangent, w_key, w_value, racks)
    grad_w_key = lax.psum(part_key, "db").astype(F32)
    grad_w_value = lax.psum(part_value, "db").astype(F32)
    shares = lax.psum_scatter(use_grad, "rack", scatter_dimension=0, tiled=True)[0]
    outgoing = pick(placed.T, shares)
    returned = lax.all_to_all(outgoing.reshape(peer_count, CAP, rows, width), "db", split_axis=0, concat_axis=0, tiled=True)
    grad_database = pick(selector.T, returned.reshape(peer_count * CAP, rows, width))
    return attended, grad_query, grad_w_key, grad_w_value, grad_database


def solution(mesh):
    return jax.shard_map(
        local,
        mesh=mesh,
        in_specs=(
            P("db", "rack"), P("db", "rack"), P("db", None, None), P(None, "rack"), P(None, "rack"), P("db", None), P("db", None),
        ),
        out_specs=(P("db", "rack"), P("db", "rack"), P(None, "rack"), P(None, "rack"), P("db", "rack", None)),
        check_vma=False,
    )
```

time: 481 us -> 322 us (0.67); the launches traced: 474 us -> 321 us
  matrix products: 133 us -> 3.76 us
  Pallas kernels: 0 us -> 71.9 us
  local copies, waits for them, and re-layouts: 64.3 us -> 11.1 us
  waiting for transfers between devices: 207 us -> 175 us
  other arithmetic: 25.8 us -> 7.77 us
  blocking collectives: 15.5 us -> 22.6 us
    all_to_all x2, waiting for transfers between devices: 156 us -> 6.16 us  [the longest x1 6.16 us: local(): lax.all_to_all(wanted.reshape(peer_count, CAP), 'db', split_axis=0, conca...]
    dot_general x13 -> x4, matrix products: 133 us -> 3.76 us  [pick(): jnp.einsum('ns,spw->npw', selector, source, preferred_element_type=F32)]
    psum x1, waiting for transfers between devices: 26.4 us -> 104 us  [local(): grad_w_key = lax.psum(part_key, 'db').astype(F32)]
    pallas_call x0 -> x1, Pallas kernels: none -> 71.9 us  [block_call(): pl.pallas_call(functools.partial(block_kernel, spans, heads), grid=(heads...]
    all_gather x0 -> x1, waiting for transfers between devices: none -> 27.4 us  [local(): panels = lax.all_gather(mine, 'rack', axis=1, tiled=True)]
    gather x2 -> x0, local copies, waits for them, and re-layouts: 16.8 us -> none  [the longest x1 9.91 us: local(): jnp.take(database, picked, axis=0)]
    reshape x4 -> x0, local copies, waits for them, and re-layouts: 16.7 us -> none  [the longest x1 7.44 us: local(): value_uses = grad_value.reshape(use_count, panel_len, features)]
    select_n x5 -> x0, other arithmetic: 14.9 us -> none  [the longest x2 9.9 us: local(): jnp.take(database, picked, axis=0)]
  transfers between devices with their start and end apart: 4 -> 5, of which waited for: 3 -> 4; matrix products, arithmetic and copies ran while one was open for 16% -> 3% of each run, Pallas kernels for 0% -> 0%
where the time goes in v1:
time: 322 us; the launch traced here: 321 us
  waiting for transfers between devices  175 us (54%)
  Pallas kernels  71.9 us (22%)
  blocking collectives  22.6 us (7%)
  starting transfers between devices  15.2 us (5%)
  between operations  13.8 us (4%)
  local copies, waits for them, and re-layouts  11.1 us (3%)
  other arithmetic  7.77 us (2%)
  matrix products  3.76 us (1%)
    psum x1, waiting for transfers between devices, local(): grad_w_key = lax.psum(part_key, 'db').astype(F32)  104 us
    pallas_call x1, Pallas kernels, block_call(): pl.pallas_call(functools.partial(block_kernel, spans, heads), grid=(heads...  71.9 us
    reduce_scatter x1, waiting for transfers between devices, local(): lax.psum_scatter(use_grad, 'rack', scatter_dimension=0, tiled=True)[0]  36.1 us
    all_gather x1, waiting for transfers between devices, local(): panels = lax.all_gather(mine, 'rack', axis=1, tiled=True)  27.4 us
    all_to_all x1, blocking collectives, local(): lax.all_to_all(answer, 'db', split_axis=0, concat_axis=0, tiled=True)  22.6 us
    all_to_all x1, starting transfers between devices, local(): lax.all_to_all(wanted.reshape(peer_count, CAP), 'db', split_axis=0, conca...  8.13 us
    all_to_all x1, starting transfers between devices, local(): lax.all_to_all(outgoing.reshape(peer_count, CAP, rows, width), 'db', spli...  6.98 us
  transfers between devices with their start and end apart: 5, of which 4 were waited for; matrix products, arithmetic and copies ran while one was open for 3% of the time, Pallas kernels for 0%

profile of v1, /device:TPU:0, one launch (start us, length us, event | category | flops | bytes accessed | tf_op | source)
XLA Modules:
  0.0 320.9 jit_solution(18245244888016799159)
XLA Ops:
  7.2 0.7 broadcast_add_fusion
  8.0 0.8 copy.39
  9.1 0.7 add.46
  9.8 8.1 %all-to-all-start = ((s32[16,1,3]{2,1,0:T(1,128)}), s32[16,1,3]{2,1,0:T(1,128)S(1)}, u32[]{:S(2)}, u32[]{:S(2)}) async-start(s32[16,1,3]{2,1,0:T(1,128)} %bitcast.1), calls=%async_computation | async-start | bytes 16384 | tf_op jit(solution)/shard_map/all_to_all | solution.py:144
  18.0 1.3 constant_dynamic-slice_fusion
  19.3 6.2 %all-to-all-done = s32[16,1,3]{2,1,0:T(1,128)S(1)} async-done(((s32[16,1,3]{2,1,0:T(1,128)}), s32[16,1,3]{2,1,0:T(1,128)S(1)}, u32[]{:S(2)}, u32[]{:S(2)}) %all-to-all-start) | async-done | bytes 224 | tf_op jit(solution)/shard_map/all_to_all | solution.py:144
  25.5 0.5 broadcast.43
  26.0 0.7 reduce.3
  26.7 0.6 convolution_convert_fusion.1
  27.6 22.6 %all_to_all.16 = bf16[16,3,16,896]{3,2,1,0:T(8,128)(2,1)S(1)} all-to-all(bf16[16,3,16,896]{3,2,1,0:T(8,128)(2,1)S(1)} %bitcast.16), channel_id=1, replica_groups=mesh['db'=16,'rack'=8] {'db'}, dimensions={0} | all-to-all | bytes 2752512 | tf_op jit(solution)/shard_map/all_to_all | solution.py:150
  50.2 1.2 fusion.3
  51.4 27.4 %all-gather.2.cloned.1.call-done = bf16[16,128,896]{2,0,1:T(8,128)(2,1)} async-done(((bf16[16,16,896]{2,0,1:T(8,128)(2,1)}), bf16[16,128,896]{2,0,1:T(8,128)(2,1)}) %all-gather.2.cloned.1.call-update) | async-done | bytes 3670032 | tf_op jit(solution)/shard_map/all_gather | solution.py:153
  78.8 4.7 %copy.45 = bf16[16,128,896]{2,1,0:T(8,128)(2,1)} copy(bf16[16,128,896]{2,0,1:T(8,128)(2,1)} %all-gather.2.cloned.1.call-done) | data formatting | bytes 7340032 | tf_op jit(solution)/shard_map/all_gather | solution.py:153
  83.5 71.9 %block.1 = (bf16[512,1024]{1,0:T(8,128)(2,1)}, bf16[512,1024]{1,0:T(8,128)(2,1)}, bf16[896,1024]{1,0:T(8,128)(2,1)}, bf16[896,1024]{1,0:T(8,128)(2,1)}, bf16[8,16,16,896]{3,2,1,0:T(8,128)(2,1)}) custom-call(bf16[2048,896]{1,0:T(8,128)(2,1)} %bitcast.18, bf16[512,1024]{1,0:T(8,128)(2,1)} %queries.1, bf16[512,1024]{1,0:T(8,128)(2,1)} %cotangent.1, ...), custom_call_target="tpu_custom_call" | custom-call | flops 22548578304 | bytes 25165824 | tf_op jit(solution)/shard_map/block/pallas_call | solution.py:98
  155.4 0.7 all-reduce.3.cloned.1.call-update
  156.1 36.1 %reduce-scatter.2.cloned.1.call-done = bf16[1,16,16,896]{3,2,1,0:T(8,128)(2,1)} async-done(((bf16[8,16,16,896]{3,2,1,0:T(8,128)(2,1)}), bf16[1,16,16,896]{3,2,1,0:T(8,128)(2,1)}) %reduce-scatter.2.cloned.1.call-update) | async-done | bytes 458768 | tf_op jit(solution)/shard_map/reduce_scatter | solution.py:157
  192.2 1.6 convolution_convert_fusion
  193.9 1.4 copy.47
  195.3 7.0 %all-to-all-start.2 = ((bf16[16,3,16,896]{3,2,1,0:T(8,128)(2,1)}), bf16[16,3,16,896]{3,2,1,0:T(8,128)(2,1)S(1)}, u32[]{:S(2)}, u32[]{:S(2)}) async-start(bf16[16,3,16,896]{3,2,1,0:T(8,128)(2,1)} %bitcast.7), calls=%async_computation.3 | async-start | bytes 2752512 | tf_op jit(solution)/shard_map/all_to_all | solution.py:159
  202.3 104.4 %all-reduce.3.cloned.1.call-done = (bf16[896,1024]{1,0:T(8,128)(2,1)}, bf16[896,1024]{1,0:T(8,128)(2,1)}) async-done(((bf16[896,1024]{1,0:T(8,128)(2,1)}, bf16[896,1024]{1,0:T(8,128)(2,1)}), (bf16[896,1024]{1,0:T(8,128)(2,1)}, bf16[896,1024]{1,0:T(8,128)(2,1)})) %all-reduce.3.cloned.1.call-update) | async-done | bytes 3670032 | tf_op jit(solution)/shard_map/psum | solution.py:155
  306.7 3.9 %convert_element_type.27 = f32[896,1024]{1,0:T(8,128)} convert(bf16[896,1024]{1,0:T(8,128)(2,1)} %get-tuple-element.35) | non-fusion elementwise | flops 917504 | bytes 5505024 | tf_op jit(solution)/shard_map/convert_element_type | solution.py:155
  310.6 2.3 convert_element_type.28
  312.8 0.4 convolution_convert_fusion.2
  313.2 1.2 copy.49
  (17 shorter events, 1.0 us)
Async XLA Ops:
  9.8 15.6 %all-to-all-start = ((s32[16,1,3]{2,1,0:T(1,128)}), s32[16,1,3]{2,1,0:T(1,128)S(1)}, u32[]{:S(2)}, u32[]{:S(2)}) async-start(s32[16,1,3]{2,1,0:T(1,128)} %bitcast.1), calls=%async_computation | async-start | bytes 16384 | tf_op jit(solution)/shard_map/all_to_all | solution.py:144
  18.0 60.8 %all-gather.2.cloned.1.call-start = ((), (), s32[]{:S(2)}) async-start(), calls=%async_computation.4 | async-start | bytes 4128768 | tf_op jit(solution)/shard_map/all_gather | solution.py:153
  51.3 140.9 %reduce-scatter.2.cloned.1.call-start = ((), (), s32[]{:S(2)}) async-start(), calls=%async_computation.5 | async-start | bytes 4128768 | tf_op jit(solution)/shard_map/reduce_scatter | solution.py:157
  155.4 151.3 %all-reduce.3.cloned.1.call-start = ((), (), s32[]{:S(2)}) async-start(), calls=%async_computation.6 | async-start | bytes 7340032 | tf_op jit(solution)/shard_map/psum | solution.py:155
  195.3 117.5 %all-to-all-start.2 = ((bf16[16,3,16,896]{3,2,1,0:T(8,128)(2,1)}), bf16[16,3,16,896]{3,2,1,0:T(8,128)(2,1)S(1)}, u32[]{:S(2)}, u32[]{:S(2)}) async-start(bf16[16,3,16,896]{3,2,1,0:T(8,128)(2,1)} %bitcast.7), calls=%async_computation.3 | async-start | bytes 2752512 | tf_op jit(solution)/shard_map/all_to_all | solution.py:159
  306.7 3.9 %copy-start = (bf16[896,1024]{1,0:T(8,128)(2,1)S(1)}, bf16[896,1024]{1,0:T(8,128)(2,1)}, u32[]{:S(2)}) copy-start(bf16[896,1024]{1,0:T(8,128)(2,1)} %get-tuple-element.36) | copy-start | bytes 5505028
Sparse Core Ops, SparseCore 0:
  51.5 27.2 all-gather.1
  155.5 36.6 reduce-scatter.1
  195.7 110.9 all-reduce.2

commit v2 on v1

--- a/solution.py
+++ b/solution.py
@@ -123,6 +123,335 @@
     )(panels.reshape(total, width), queries, cotangent, w_key, w_value)
 
 
+MESH = pl.DeviceIdType.MESH
+
+
+class Links:
+    def __init__(self, side_z, side_y, side_x):
+        db, rack = lax.axis_index("db"), lax.axis_index("rack")
+        self.db, self.rack = db, rack
+        self.z, self.y = db // side_y, db % side_y
+        self.x, self.core = rack // 2, rack % 2
+        self.side_x = side_x
+        self.ids = {
+            ("y", 1): (self.z * side_y + (self.y + 1) % side_y, rack),
+            ("y", -1): (self.z * side_y + (self.y + side_y - 1) % side_y, rack),
+            ("z", 1): ((self.z + 1) % side_z * side_y + self.y, rack),
+            ("z", -1): ((self.z + side_z - 1) % side_z * side_y + self.y, rack),
+            ("x", 1): (db, (self.x + 1) % side_x * 2 + self.core),
+            ("x", -1): (db, (self.x + side_x - 1) % side_x * 2 + self.core),
+            ("core", 1): (db, self.x * 2 + 1 - self.core),
+        }
+
+    def place(self, axis):
+        return {"y": self.y, "z": self.z, "x": self.x}[axis]
+
+
+class Mail:
+    def __init__(self, send_sems, recv_sems, first=0):
+        self.send_sems, self.recv_sems, self.next = send_sems, recv_sems, first
+        self.open = {}
+        self.sent = []
+
+    def send(self, name, source, target, device):
+        copy = pltpu.make_async_remote_copy(
+            src_ref=source, dst_ref=target, send_sem=self.send_sems.at[self.next], recv_sem=self.recv_sems.at[self.next],
+            device_id=device, device_id_type=MESH,
+        )
+        self.next += 1
+        copy.start()
+        self.open[name] = copy
+        self.sent.append(copy)
+
+    def arrive(self, *names):
+        for name in names:
+            self.open[name].wait_recv()
+
+    def drain(self):
+        for copy in self.sent:
+            copy.wait_send()
+        self.sent = []
+
+
+def add(*terms):
+    total = terms[0].astype(F32)
+    for term in terms[1:]:
+        total = total + term.astype(F32)
+    return total.astype(BF16)
+
+
+class Reduction:
+    def __init__(self, tag, links, mail, part, full, first_column, columns, axes, near, far, middle):
+        self.tag, self.links, self.mail = tag, links, mail
+        self.part, self.full, self.first_column, self.columns = part, full, first_column, columns
+        self.one, self.two = axes
+        self.near, self.far, self.middle = near, far, middle
+        self.rows = part.shape[0] // 4
+        self.half = self.rows // 2
+        self.narrow = columns // 4
+
+    def name(self, what):
+        return (self.tag, what)
+
+    def spot(self, ref, one, side):
+        first = one * self.rows + side * self.half
+        return ref.at[pl.ds(pl.multiple_of(first, 16), self.half), pl.ds(self.first_column, self.columns)]
+
+    def small(self, two, side):
+        return self.middle.at[pl.ds(side * self.half, self.half), pl.ds(pl.multiple_of(two * self.narrow, 128), self.narrow)]
+
+    def piece(self, one, two, first, size):
+        return self.full.at[
+            pl.ds(pl.multiple_of(one * self.rows + first, 16), size),
+            pl.ds(pl.multiple_of(self.first_column + two * self.narrow, 128), self.narrow),
+        ]
+
+    def first(self, axis, at, buffer, level):
+        links, mail, me = self.links, self.mail, self.links.place(axis)
+        up, down = links.ids[(axis, 1)], links.ids[(axis, -1)]
+        mail.send(self.name(level + "ra"), at((me + 2) % 4, 0), buffer.at[0], up)
+        mail.send(self.name(level + "rb"), at((me + 2) % 4, 1), buffer.at[1], down)
+        mail.send(self.name(level + "db"), at((me + 1) % 4, 1), buffer.at[3], up)
+        mail.send(self.name(level + "da"), at((me + 3) % 4, 0), buffer.at[2], down)
+
+    def second(self, axis, at, buffer, level):
+        links, mail, me = self.links, self.mail, self.links.place(axis)
+        up, down = links.ids[(axis, 1)], links.ids[(axis, -1)]
+        mail.arrive(self.name(level + "ra"))
+        buffer[0, :, :] = add(buffer[0], at((me + 1) % 4, 0)[...])
+        mail.send(self.name(level + "sa"), buffer.at[0], buffer.at[4], up)
+        mail.arrive(self.name(level + "rb"))
+        buffer[1, :, :] = add(buffer[1], at((me + 3) % 4, 1)[...])
+        mail.send(self.name(level + "sb"), buffer.at[1], buffer.at[5], down)
+
+    def third(self, axis, at, buffer, level, side):
+        mail, me = self.mail, self.links.place(axis)
+        letter = "ab"[side]
+        mail.arrive(self.name(level + "d" + letter), self.name(level + "s" + letter))
+        return add(buffer[2 + side], buffer[4 + side], at(me, side)[...])
+
+    def spread(self, axis, at, level):
+        links, mail, me = self.links, self.mail, self.links.place(axis)
+        mail.send(self.name(level + "up"), at(me, 0, self.rows), at(me, 0, self.rows), links.ids[(axis, 1)])
+        mail.send(self.name(level + "down"), at(me, 0, self.rows), at(me, 0, self.rows), links.ids[(axis, -1)])
+
+    def forward(self, axis, at, level):
+        links, mail, me = self.links, self.mail, self.links.place(axis)
+        mail.arrive(self.name(level + "up"))
+        mail.send(
+            self.name(level + "on"), at((me + 3) % 4, 0, self.half), at((me + 3) % 4, 0, self.half), links.ids[(axis, 1)]
+        )
+        mail.arrive(self.name(level + "down"))
+        mail.send(
+            self.name(level + "back"), at((me + 1) % 4, self.half, self.half), at((me + 1) % 4, self.half, self.half),
+            links.ids[(axis, -1)],
+        )
+
+    def stage(self, number):
+        wide = lambda one, side: self.spot(self.part, one, side)
+        mine = self.links.place(self.one)
+        column = lambda two, first, size: self.piece(mine, two, first, size)
+        row = lambda one, first, size: self.full.at[
+            pl.ds(pl.multiple_of(one * self.rows + first, 16), size), pl.ds(self.first_column, self.columns)
+        ]
+        if number == 0:
+            self.first(self.one, wide, self.near, "n")
+        elif number == 1:
+            self.second(self.one, wide, self.near, "n")
+        elif number == 2:
+            for side in (0, 1):
+                self.middle[side * self.half:(side + 1) * self.half, :] = self.third(self.one, wide, self.near, "n", side)
+            self.first(self.two, self.small, self.far, "f")
+        elif number == 3:
+            self.second(self.two, self.small, self.far, "f")
+        elif number == 4:
+            for side in (0, 1):
+                total = self.third(self.two, self.small, self.far, "f", side)
+                column(self.links.place(self.two), side * self.half, self.half)[...] = total
+            self.spread(self.two, column, "g")
+        elif number == 5:
+            self.forward(self.two, column, "g")
+        elif number == 6:
+            self.mail.arrive(self.name("gon"), self.name("gback"))
+            self.spread(self.one, row, "h")
+        elif number == 7:
+            self.forward(self.one, row, "h")
+        else:
+            self.mail.arrive(self.name("hon"), self.name("hback"))
+
+
+class Return:
+    def __init__(self, links, mail, use_grad, user, returned, crossed, ring, mine, leaving, leave_sems, land_sems):
+        self.links, self.mail, self.use_grad, self.user, self.returned = links, mail, use_grad, user, returned
+        self.crossed, self.ring, self.mine, self.leaving = crossed, ring, mine, leaving
+        self.leave_sems, self.land_sems = leave_sems, land_sems
+        self.half = mine.shape[0] // 2
+
+    def spot(self, far, side):
+        return self.crossed.at[(self.links.x + far) % 4, pl.ds(side * self.half, self.half)]
+
+    def stage(self, number):
+        links, mail = self.links, self.mail
+        up, down = links.ids[("x", 1)], links.ids[("x", -1)]
+        half = self.half
+        if number == 0:
+            for far in (2, 1, 3, 0):
+                x = (links.x + far) % 4
+                mail.send(("c", far), self.use_grad.at[x * 2 + 1 - links.core], self.crossed.at[x], links.ids[("core", 1)])
+        elif number == 1:
+            def join(far):
+                x = (links.x + far) % 4
+                mail.arrive(("c", far))
+
+                @pl.loop(0, half * 2)
+                def _(n):
+                    self.crossed[x, n] = add(self.crossed[x, n], self.use_grad[x * 2 + links.core, n])
+
+            join(2)
+            mail.send("xra", self.spot(2, 0), self.ring.at[0], up)
+            mail.send("xrb", self.spot(2, 1), self.ring.at[1], down)
+            join(1)
+            mail.send("xdb", self.spot(1, 1), self.ring.at[3], up)
+            join(3)
+            mail.send("xda", self.spot(3, 0), self.ring.at[2], down)
+            join(0)
+        elif number == 2:
+            for side, letter, far, device in ((0, "a", 1, up), (1, "b", 3, down)):
+                mail.arrive("xr" + letter)
+                own = self.spot(far, side)
+
+                @pl.loop(0, half)
+                def _(n):
+                    self.ring[side, n] = add(self.ring[side, n], own[n])
+
+                mail.send("xs" + letter, self.ring.at[side], self.ring.at[4 + side], device)
+        elif number == 3:
+            for side, letter in ((0, "a"), (1, "b")):
+                mail.arrive("xd" + letter, "xs" + letter)
+                own = self.spot(0, side)
+
+                @pl.loop(0, half)
+                def _(n):
+                    self.mine[side * half + n] = add(self.ring[2 + side, n], self.ring[4 + side, n], own[n])
+
+            self.mine[2 * half] = jnp.zeros(self.mine.shape[1:], BF16)
+            peers = self.returned.shape[0]
+
+            def fill(peer, target, at):
+                for k in range(CAP):
+                    target[at, k] = self.mine[self.user[peer * CAP + k]]
+
+            fill(links.db, self.returned, links.db)
+
+            @pl.loop(1, peers)
+            def _(far):
+                peer = (links.db + far) % peers
+                fill(peer, self.leaving, peer)
+                self.copy(far).start()
+        else:
+            @pl.loop(1, self.returned.shape[0])
+            def _(far):
+                self.copy(far).wait()
+
+    def copy(self, far):
+        links = self.links
+        peer = (links.db + far) % self.returned.shape[0]
+        return pltpu.make_async_remote_copy(
+            src_ref=self.leaving.at[peer], dst_ref=self.returned.at[links.db], send_sem=self.leave_sems.at[far],
+            recv_sem=self.land_sems.at[far], device_id=(peer, links.rack), device_id_type=MESH,
+        )
+
+
+def greet(links, peers):
+    barrier = pltpu.get_barrier_semaphore()
+    others = [links.ids[("core", 1)], links.ids[("x", 1)], links.ids[("x", -1)]]
+    for device in others:
+        pl.semaphore_signal(barrier, inc=1, device_id=device, device_id_type=MESH)
+
+    @pl.loop(1, peers)
+    def _(far):
+        pl.semaphore_signal(barrier, inc=1, device_id=((links.db + far) % peers, links.rack), device_id_type=MESH)
+
+    pl.semaphore_wait(barrier, len(others) + peers - 1)
+
+
+GROUPS = 2
+MESSAGES = 20 * 2 * GROUPS + 10
+
+
+def return_kernel(user, part_key, part_value, use_grad, full_key, full_value, returned, near, far, middle, crossed, ring, mine,
+                  leaving, send_sems, recv_sems, leave_sems, land_sems):
+    links = Links(4, 4, 4)
+    greet(links, returned.shape[0])
+    mail = Mail(send_sems, recv_sems)
+    columns = part_key.shape[1] // GROUPS
+    items = []
+    for g in range(GROUPS):
+        for m, (part, full, axes) in enumerate(((part_key, full_key, "yz"), (part_value, full_value, "zy"))):
+            n = g * 2 + m
+            items.append(Reduction(n, links, mail, part, full, g * columns, columns, axes, near.at[n], far.at[n], middle.at[n]))
+    back = Return(links, mail, use_grad, user, returned, crossed, ring, mine, leaving, leave_sems, land_sems)
+    back.stage(0)
+    for item in items:
+        item.stage(0)
+    back.stage(1)
+    for item in items[:2]:
+        item.stage(1)
+    back.stage(2)
+    for item in items[:2]:
+        item.stage(2)
+    for item in items[2:]:
+        item.stage(1)
+    back.stage(3)
+    for item in items[:2]:
+        item.stage(3)
+    for item in items[2:]:
+        item.stage(2)
+    for number in (4, 5, 6, 7, 8):
+        for item in items[:2]:
+            item.stage(number)
+        for item in items[2:]:
+            item.stage(number - 1)
+    for item in items[2:]:
+        item.stage(8)
+    back.stage(4)
+    mail.drain()
+
+
+def return_call(user, part_key, part_value, use_grad, peers):
+    width, features = part_key.shape
+    racks, uses, rows, _ = use_grad.shape
+    columns = features // GROUPS
+    vmem = pl.BlockSpec(memory_space=pltpu.VMEM)
+    return pl.pallas_call(
+        return_kernel,
+        out_shape=(
+            jax.ShapeDtypeStruct((width, features), BF16),
+            jax.ShapeDtypeStruct((width, features), BF16),
+            jax.ShapeDtypeStruct((peers, CAP, rows, width), BF16),
+        ),
+        in_specs=[pl.BlockSpec(memory_space=pltpu.SMEM), vmem, vmem, vmem],
+        out_specs=(vmem, vmem, vmem),
+        scratch_shapes=[
+            pltpu.VMEM((2 * GROUPS, 6, width // 8, columns), BF16),
+            pltpu.VMEM((2 * GROUPS, 6, width // 8, columns // 4), BF16),
+            pltpu.VMEM((2 * GROUPS, width // 4, columns), BF16),
+            pltpu.VMEM((4, uses, rows, width), BF16),
+            pltpu.VMEM((6, uses // 2, rows, width), BF16),
+            pltpu.VMEM((uses + 1, rows, width), BF16),
+            pltpu.VMEM((peers, CAP, rows, width), BF16),
+            pltpu.SemaphoreType.DMA((MESSAGES,)),
+            pltpu.SemaphoreType.DMA((MESSAGES,)),
+            pltpu.SemaphoreType.DMA((peers,)),
+            pltpu.SemaphoreType.DMA((peers,)),
+        ],
+        compiler_params=pltpu.CompilerParams(
+            collective_id=1, has_side_effects=True, vmem_limit_bytes=48 * 1024 * 1024
+        ),
+        name="send_back",
+    )(user, part_key, part_value, use_grad)
+
+
 def pick(selector, source):
     return jnp.einsum("ns,spw->npw", selector, source, preferred_element_type=F32).astype(BF16)
 
@@ -141,6 +470,7 @@
     target = owners * CAP + ranked
     named = (target[None, :] == jnp.arange(peer_count * CAP, dtype=jnp.int32)[:, None]).astype(jnp.int32)
     wanted = jnp.sum(named * (offsets - local_rows)[None, :], axis=1) + local_rows
+    user = jnp.sum(named * (jnp.arange(use_count, dtype=jnp.int32) - use_count)[None, :], axis=1) + use_count
     asked_rows = lax.all_to_all(wanted.reshape(peer_count, CAP), "db", split_axis=0, concat_axis=0, tiled=True)
     own = lax.dynamic_slice_in_dim(database, lax.axis_index("rack") * rows, rows, 1)
     selector = (
@@ -152,11 +482,8 @@
     mine = pick(placed, arrived.reshape(peer_count * CAP, rows, width))
     panels = lax.all_gather(mine, "rack", axis=1, tiled=True)
     attended, grad_query, part_key, part_value, use_grad = block_call(panels, queries, cotangent, w_key, w_value, racks)
-    grad_w_key = lax.psum(part_key, "db").astype(F32)
-    grad_w_value = lax.psum(part_value, "db").astype(F32)
-    shares = lax.psum_scatter(use_grad, "rack", scatter_dimension=0, tiled=True)[0]
-    outgoing = pick(placed.T, shares)
-    returned = lax.all_to_all(outgoing.reshape(peer_count, CAP, rows, width), "db", split_axis=0, concat_axis=0, tiled=True)
+    full_key, full_value, returned = return_call(user, part_key, part_value, use_grad, peer_count)
+    grad_w_key, grad_w_value = full_key.astype(F32), full_value.astype(F32)
     grad_database = pick(selector.T, returned.reshape(peer_count * CAP, rows, width))
     return attended, grad_query, grad_w_key, grad_w_value, grad_database
 

time: 322 us -> 244 us (0.76)
  waiting for transfers between devices: 175 us -> 33.6 us
  Pallas kernels: 71.9 us -> 147 us
  starting transfers between devices: 15.2 us -> 8.17 us
    psum x1 -> x0, waiting for transfers between devices: 104 us -> none  [local(): grad_w_key = lax.psum(part_key, 'db').astype(F32)]
    pallas_call x0 -> x1, Pallas kernels: none -> 75.5 us  [return_call(): pl.pallas_call(return_kernel, out_shape=(jax.ShapeDtypeStruct((width, fea...]
    reduce_scatter x1 -> x0, waiting for transfers between devices: 36.1 us -> none  [local(): lax.psum_scatter(use_grad, 'rack', scatter_dimension=0, tiled=True)[0]]
    all_to_all x1 -> x0, starting transfers between devices: 6.98 us -> none  [local(): lax.all_to_all(outgoing.reshape(peer_count, CAP, rows, width), 'db', spli...]
  transfers between devices with their start and end apart: 5 -> 2, of which waited for: 4 -> 2; matrix products, arithmetic and copies ran while one was open for 3% -> 1% of each run, Pallas kernels for 0% -> 0%
where the time goes in v2:
time: 244 us
  Pallas kernels  147 us (60%)
  waiting for transfers between devices  33.6 us (14%)
  blocking collectives  22.6 us (9%)
  between operations  14.1 us (6%)
  local copies, waits for them, and re-layouts  9.74 us (4%)
  starting transfers between devices  8.17 us (3%)
  other arithmetic  6.15 us (3%)
    pallas_call x1, Pallas kernels, return_call(): pl.pallas_call(return_kernel, out_shape=(jax.ShapeDtypeStruct((width, fea...  75.5 us
    pallas_call x1, Pallas kernels, block_call(): pl.pallas_call(functools.partial(block_kernel, spans, heads), grid=(heads...  71.9 us
    all_gather x1, waiting for transfers between devices, local(): panels = lax.all_gather(mine, 'rack', axis=1, tiled=True)  27.4 us
    all_to_all x1, blocking collectives, local(): lax.all_to_all(answer, 'db', split_axis=0, concat_axis=0, tiled=True)  22.6 us
    all_to_all x1, starting transfers between devices, local(): lax.all_to_all(wanted.reshape(peer_count, CAP), 'db', split_axis=0, conca...  8.13 us
    all_to_all x1, waiting for transfers between devices, local(): lax.all_to_all(wanted.reshape(peer_count, CAP), 'db', split_axis=0, conca...  6.16 us
  transfers between devices with their start and end apart: 2, of which 2 were waited for; matrix products, arithmetic and copies ran while one was open for 1% of the time, Pallas kernels for 0%

profile of v2, /device:TPU:0, one launch (start us, length us, event | category | flops | bytes accessed | tf_op | source)
XLA Modules:
  0.0 243.9 jit_solution(10947518943146052850)
XLA Ops:
  7.2 0.7 broadcast_add_fusion
  7.9 0.1 copy.36
  8.0 0.8 copy.35
  8.9 0.2 convert_reduce_fusion
  9.1 0.1 select_reduce_fusion
  9.2 0.7 add.51
  9.9 8.1 %all-to-all-start = ((s32[16,1,3]{2,1,0:T(1,128)}), s32[16,1,3]{2,1,0:T(1,128)S(1)}, u32[]{:S(2)}, u32[]{:S(2)}) async-start(s32[16,1,3]{2,1,0:T(1,128)} %bitcast.1), calls=%async_computation | async-start | bytes 16384 | tf_op jit(solution)/shard_map/all_to_all | solution.py:474
  18.0 1.3 constant_dynamic-slice_fusion
  19.3 6.2 %all-to-all-done = s32[16,1,3]{2,1,0:T(1,128)S(1)} async-done(((s32[16,1,3]{2,1,0:T(1,128)}), s32[16,1,3]{2,1,0:T(1,128)S(1)}, u32[]{:S(2)}, u32[]{:S(2)}) %all-to-all-start) | async-done | bytes 224 | tf_op jit(solution)/shard_map/all_to_all | solution.py:474
  25.5 0.5 broadcast.55
  26.0 0.7 reduce.3
  26.7 0.1 eq.63
  26.7 0.6 convolution_convert_fusion
  27.3 0.3 copy.39
  27.6 22.6 %all_to_all.11 = bf16[16,3,16,896]{3,2,1,0:T(8,128)(2,1)S(1)} all-to-all(bf16[16,3,16,896]{3,2,1,0:T(8,128)(2,1)S(1)} %bitcast.14), channel_id=1, replica_groups=mesh['db'=16,'rack'=8] {'db'}, dimensions={0} | all-to-all | bytes 2752512 | tf_op jit(solution)/shard_map/all_to_all | solution.py:480
  50.2 1.2 fusion.3
  51.4 27.4 %all-gather.2.cloned.1.call-done = bf16[16,128,896]{2,0,1:T(8,128)(2,1)} async-done(((bf16[16,16,896]{2,0,1:T(8,128)(2,1)}), bf16[16,128,896]{2,0,1:T(8,128)(2,1)}) %all-gather.2.cloned.1.call-update) | async-done | bytes 3670032 | tf_op jit(solution)/shard_map/all_gather | solution.py:483
  78.8 4.7 %copy.41 = bf16[16,128,896]{2,1,0:T(8,128)(2,1)} copy(bf16[16,128,896]{2,0,1:T(8,128)(2,1)} %all-gather.2.cloned.1.call-done) | data formatting | bytes 7340032 | tf_op jit(solution)/shard_map/all_gather | solution.py:483
  83.5 71.9 %block.1 = (bf16[512,1024]{1,0:T(8,128)(2,1)}, bf16[512,1024]{1,0:T(8,128)(2,1)}, bf16[896,1024]{1,0:T(8,128)(2,1)}, bf16[896,1024]{1,0:T(8,128)(2,1)}, bf16[8,16,16,896]{3,2,1,0:T(8,128)(2,1)}) custom-call(bf16[2048,896]{1,0:T(8,128)(2,1)} %bitcast.15, bf16[512,1024]{1,0:T(8,128)(2,1)} %queries.1, bf16[512,1024]{1,0:T(8,128)(2,1)} %cotangent.1, ...), custom_call_target="tpu_custom_call" | custom-call | flops 22548578304 | bytes 25165824 | tf_op jit(solution)/shard_map/block/pallas_call | solution.py:98
  155.5 75.5 %send_back.1 = (bf16[896,1024]{1,0:T(8,128)(2,1)S(1)}, bf16[896,1024]{1,0:T(8,128)(2,1)S(1)}, bf16[16,3,16,896]{3,2,1,0:T(8,128)(2,1)S(1)}) custom-call(s32[48]{0:T(128)S(1)} %get-tuple-element.43.user, bf16[896,1024]{1,0:T(8,128)(2,1)} %get-tuple-element.15.part_key, bf16[896,1024]{1,0:T(8,128)(2,1)} %get-tuple-element.16.part_value, ...), custom_call_target="tpu_custom_call" | custom-call | tf_op jit(solution)/shard_map/send_back/pallas_call | solution.py:426
  230.9 0.4 convolution_convert_fusion.1
  231.3 1.2 copy.43
  232.6 2.2 convert_element_type.24
  234.8 2.2 convert_element_type.25
  (7 shorter events, 0.2 us)
Async XLA Ops:
  9.9 15.6 %all-to-all-start = ((s32[16,1,3]{2,1,0:T(1,128)}), s32[16,1,3]{2,1,0:T(1,128)S(1)}, u32[]{:S(2)}, u32[]{:S(2)}) async-start(s32[16,1,3]{2,1,0:T(1,128)} %bitcast.1), calls=%async_computation | async-start | bytes 16384 | tf_op jit(solution)/shard_map/all_to_all | solution.py:474
  18.0 60.8 %all-gather.2.cloned.1.call-start = ((), (), s32[]{:S(2)}) async-start(), calls=%async_computation.2 | async-start | bytes 4128768 | tf_op jit(solution)/shard_map/all_gather | solution.py:483
Sparse Core Ops, SparseCore 0:
  51.5 27.2 all-gather.1

commit v3 on v2

--- a/solution.py
+++ b/solution.py
@@ -339,7 +339,7 @@
 
             def fill(peer, target, at):
                 for k in range(CAP):
-                    target[at, k] = self.mine[self.user[peer * CAP + k]]
+                    target[at, k] = self.mine[self.user[peer, 0, k]]
 
             fill(links.db, self.returned, links.db)
 
@@ -452,6 +452,160 @@
     )(user, part_key, part_value, use_grad)
 
 
+def fetch_kernel(cuts, owners, slots, database, panels, asked, user, stored, wanted, heard, leaving, landing, mine, load_sem, ask_send,
+                 ask_recv, leave_sems, land_sems, own_sems, send_sems, recv_sems):
+    links = Links(4, 4, 4)
+    peers = asked.shape[0]
+    local_rows, _, width = stored.shape
+    uses, rows = mine.shape[0], mine.shape[1]
+    nbrs = owners.shape[1]
+    my_rows = lambda x, core: pl.ds(pl.multiple_of((x * 2 + core) * rows, rows), rows)
+    load = pltpu.make_async_copy(database.at[:, my_rows(links.x, links.core), :], stored, load_sem.at[0])
+    load.start()
+    greet(links, peers)
+
+    peer_of = lax.broadcasted_iota(jnp.int32, (peers, 1, 128), 0)
+    lane = lax.broadcasted_iota(jnp.int32, (peers, 1, 128), 2)
+    seen = jnp.zeros((peers, 1, 128), jnp.int32)
+    rows_wanted = jnp.full((peers, 1, 128), local_rows, jnp.int32)
+    users = jnp.full((peers, 1, 128), uses, jnp.int32)
+    for u in range(uses):
+        named = peer_of == owners[u // nbrs, u % nbrs]
+        here = named & (lane == seen)
+        rows_wanted = jnp.where(here, slots[u // nbrs, u % nbrs], rows_wanted)
+        users = jnp.where(here, u, users)
+        seen = seen + named.astype(jnp.int32)
+    wanted[...] = rows_wanted
+    user[...] = users
+
+    def ask(far):
+        peer = (links.db + far) % peers
+        return pltpu.make_async_remote_copy(
+            src_ref=wanted.at[peer], dst_ref=asked.at[links.db], send_sem=ask_send.at[far], recv_sem=ask_recv.at[far],
+            device_id=(peer, links.rack), device_id_type=MESH,
+        )
+
+    pl.loop(1, peers)(lambda far: ask(far).start())
+    asked[links.db] = wanted[links.db]
+    load.wait()
+    pl.loop(1, peers)(lambda far: ask(far).wait())
+    tables = pltpu.make_async_copy(asked, heard, load_sem.at[1])
+    tables.start()
+    tables.wait()
+
+    def answer(c, far):
+        peer = (links.db + far) % peers
+        return pltpu.make_async_remote_copy(
+            src_ref=leaving[c].at[peer], dst_ref=landing[c].at[links.db], send_sem=leave_sems.at[c, far],
+            recv_sem=land_sems.at[c, far], device_id=(peer, links.rack), device_id_type=MESH,
+        )
+
+    def fill(c, peer, target):
+        for k in range(CAP):
+            row = jnp.minimum(heard[peer, 0, k], local_rows - 1)
+            target[peer, k] = stored[row, :, cuts[c]:cuts[c + 1]]
+
+    for c in range(len(cuts) - 1):
+        @pl.loop(1, peers)
+        def _(far):
+            fill(c, (links.db + far) % peers, leaving[c])
+            answer(c, far).start()
+
+        fill(c, links.db, landing[c])
+
+    mail = Mail(send_sems, recv_sems)
+    up, down, across = links.ids[("x", 1)], links.ids[("x", -1)], links.ids[("core", 1)]
+    own_copies = []
+    half = uses // 2
+
+    def out(c, far, first, size):
+        return panels.at[pl.ds(first, size), my_rows((links.x + far) % 4, links.core), pl.ds(cuts[c], cuts[c + 1] - cuts[c])]
+
+    def pass_on(name, c, far, first, size, device):
+        mail.send((name, c), out(c, far, first, size), out(c, far, first, size), device)
+
+    def exchange(c):
+        mail.arrive(("up", c))
+        pass_on("on", c, 3, 0, half, up)
+        pass_on("cross3", c, 3, 0, uses, across)
+        mail.arrive(("down", c))
+        pass_on("back", c, 1, half, half, down)
+        pass_on("cross1", c, 1, 0, uses, across)
+
+    def finish(c):
+        mail.arrive(("on", c))
+        pass_on("cross2a", c, 2, 0, half, across)
+        mail.arrive(("back", c))
+        pass_on("cross2b", c, 2, half, half, across)
+
+    count = len(cuts) - 1
+    for c in range(count):
+        pl.loop(1, peers)(lambda far: answer(c, far).wait())
+        for u in range(uses):
+            owner = owners[u // nbrs, u % nbrs]
+            rank = jnp.int32(0)
+            for v in range(u):
+                rank = rank + (owners[v // nbrs, v % nbrs] == owner).astype(jnp.int32)
+            mine[u, :, cuts[c]:cuts[c + 1]] = landing[c][owner, jnp.minimum(rank, CAP - 1)]
+        source = mine.at[:, :, pl.ds(cuts[c], cuts[c + 1] - cuts[c])]
+        target = out(c, 0, 0, uses)
+        mail.send(("up", c), source, target, up)
+        mail.send(("down", c), source, target, down)
+        mail.send(("cross0", c), source, target, across)
+        copy = pltpu.make_async_copy(source, target, own_sems.at[c])
+        copy.start()
+        own_copies.append(copy)
+        if c > 0:
+            exchange(c - 1)
+    exchange(count - 1)
+    for c in range(count):
+        finish(c)
+    for c in range(count):
+        mail.arrive(("cross0", c), ("cross1", c), ("cross3", c), ("cross2a", c), ("cross2b", c))
+    for copy in own_copies:
+        copy.wait()
+    mail.drain()
+
+
+CUTS = (0, 512, 896)
+
+
+def fetch_call(owners, slots, database, peers, racks):
+    uses = owners.shape[0] * owners.shape[1]
+    local_rows, panel_len, width = database.shape
+    rows = panel_len // racks
+    parts = len(CUTS) - 1
+    chunk = lambda c: pltpu.VMEM((peers, CAP, rows, CUTS[c + 1] - CUTS[c]), BF16)
+    vmem = pl.BlockSpec(memory_space=pltpu.VMEM)
+    smem = pl.BlockSpec(memory_space=pltpu.SMEM)
+    anywhere = pl.BlockSpec(memory_space=pl.ANY)
+    sems = pltpu.SemaphoreType.DMA
+    return pl.pallas_call(
+        functools.partial(fetch_kernel, CUTS),
+        out_shape=(
+            jax.ShapeDtypeStruct((uses, panel_len, width), BF16),
+            jax.ShapeDtypeStruct((peers, 1, 128), jnp.int32),
+            jax.ShapeDtypeStruct((peers, 1, 128), jnp.int32),
+        ),
+        in_specs=[smem, smem, anywhere],
+        out_specs=(anywhere, vmem, vmem),
+        scratch_shapes=[
+            pltpu.VMEM((local_rows, rows, width), BF16),
+            pltpu.VMEM((peers, 1, 128), jnp.int32),
+            pltpu.SMEM((peers, 1, 128), jnp.int32),
+            [chunk(c) for c in range(parts)],
+            [chunk(c) for c in range(parts)],
+            pltpu.VMEM((uses, rows, width), BF16),
+            sems((2,)), sems((peers,)), sems((peers,)), sems((parts, peers)), sems((parts, peers)), sems((parts,)),
+            sems((9 * parts,)), sems((9 * parts,)),
+        ],
+        compiler_params=pltpu.CompilerParams(
+            collective_id=0, has_side_effects=True, vmem_limit_bytes=24 * 1024 * 1024
+        ),
+        name="fetch",
+    )(owners, slots, database)
+
+
 def pick(selector, source):
     return jnp.einsum("ns,spw->npw", selector, source, preferred_element_type=F32).astype(BF16)
 
@@ -459,28 +613,11 @@
 def local(queries, cotangent, database, w_key, w_value, neighbour_owner, neighbour_slot):
     peer_count = lax.axis_size("db")
     racks = lax.axis_size("rack")
-    span_count, nbr_count = neighbour_owner.shape
-    use_count = span_count * nbr_count
-    local_rows, panel_len, width = database.shape
-    rows = panel_len // racks
-    owners = neighbour_owner.reshape(use_count)
-    offsets = neighbour_slot.reshape(use_count)
-    earlier = jnp.arange(use_count)[None, :] < jnp.arange(use_count)[:, None]
-    ranked = jnp.sum(((owners[:, None] == owners[None, :]) & earlier).astype(jnp.int32), axis=1)
-    target = owners * CAP + ranked
-    named = (target[None, :] == jnp.arange(peer_count * CAP, dtype=jnp.int32)[:, None]).astype(jnp.int32)
-    wanted = jnp.sum(named * (offsets - local_rows)[None, :], axis=1) + local_rows
-    user = jnp.sum(named * (jnp.arange(use_count, dtype=jnp.int32) - use_count)[None, :], axis=1) + use_count
-    asked_rows = lax.all_to_all(wanted.reshape(peer_count, CAP), "db", split_axis=0, concat_axis=0, tiled=True)
-    own = lax.dynamic_slice_in_dim(database, lax.axis_index("rack") * rows, rows, 1)
-    selector = (
-        asked_rows.reshape(peer_count * CAP)[:, None] == jnp.arange(local_rows, dtype=jnp.int32)[None, :]
-    ).astype(BF16)
-    answer = pick(selector, own).reshape(peer_count, CAP, rows, width)
-    arrived = lax.all_to_all(answer, "db", split_axis=0, concat_axis=0, tiled=True)
-    placed = (target[:, None] == jnp.arange(peer_count * CAP, dtype=jnp.int32)[None, :]).astype(BF16)
-    mine = pick(placed, arrived.reshape(peer_count * CAP, rows, width))
-    panels = lax.all_gather(mine, "rack", axis=1, tiled=True)
+    local_rows, _, width = database.shape
+    rows = database.shape[1] // racks
+    panels, asked, user = fetch_call(neighbour_owner, neighbour_slot, database, peer_count, racks)
+    asked_rows = asked[:, 0, :CAP].reshape(peer_count * CAP)
+    selector = (asked_rows[:, None] == jnp.arange(local_rows, dtype=jnp.int32)[None, :]).astype(BF16)
     attended, grad_query, part_key, part_value, use_grad = block_call(panels, queries, cotangent, w_key, w_value, racks)
     full_key, full_value, returned = return_call(user, part_key, part_value, use_grad, peer_count)
     grad_w_key, grad_w_value = full_key.astype(F32), full_value.astype(F32)

time: 244 us -> 206 us (0.84)
  Pallas kernels: 147 us -> 193 us
  waiting for transfers between devices: 33.6 us -> 0 us
  blocking collectives: 22.6 us -> 0 us
  between operations: 14.1 us -> 0.67 us
  starting transfers between devices: 8.17 us -> 0 us
    pallas_call x0 -> x1, Pallas kernels: none -> 45.4 us  [fetch_call(): pl.pallas_call(functools.partial(fetch_kernel, CUTS), out_shape=(jax.Shap...]
    all_gather x1 -> x0, waiting for transfers between devices: 27.4 us -> none  [local(): panels = lax.all_gather(mine, 'rack', axis=1, tiled=True)]
    all_to_all x1 -> x0, blocking collectives: 22.6 us -> none  [local(): lax.all_to_all(answer, 'db', split_axis=0, concat_axis=0, tiled=True)]
    all_to_all x1 -> x0, starting transfers between devices: 8.13 us -> none  [local(): lax.all_to_all(wanted.reshape(peer_count, CAP), 'db', split_axis=0, conca...]
    all_to_all x1 -> x0, waiting for transfers between devices: 6.16 us -> none  [local(): lax.all_to_all(wanted.reshape(peer_count, CAP), 'db', split_axis=0, conca...]
    unnamed x2 -> x7, local copies, waits for them, and re-layouts: 1.96 us -> 7.65 us
    all_gather x1 -> x0, local copies, waits for them, and re-layouts: 4.73 us -> none  [local(): panels = lax.all_gather(mine, 'rack', axis=1, tiled=True)]
  transfers between devices with their start and end apart: 2 -> 0, of which waited for: 2 -> 0; matrix products, arithmetic and copies ran while one was open for 1% -> 0% of each run, Pallas kernels for 0% -> 0%
where the time goes in v3:
time: 206 us
  Pallas kernels  193 us (94%)
  local copies, waits for them, and re-layouts  7.76 us (4%)
  other arithmetic  4.5 us (2%)
    pallas_call x1, Pallas kernels, return_call(): pl.pallas_call(return_kernel, out_shape=(jax.ShapeDtypeStruct((width, fea...  75.3 us
    pallas_call x1, Pallas kernels, block_call(): pl.pallas_call(functools.partial(block_kernel, spans, heads), grid=(heads...  71.9 us
    pallas_call x1, Pallas kernels, fetch_call(): pl.pallas_call(functools.partial(fetch_kernel, CUTS), out_shape=(jax.Shap...  45.4 us
    unnamed x7, local copies, waits for them, and re-layouts  7.65 us
    convert_element_type x2, other arithmetic, local(): grad_w_key, grad_w_value = (full_key.astype(F32), full_value.astype(F32))  4.5 us

profile of v3, /device:TPU:0, one launch (start us, length us, event | category | flops | bytes accessed | tf_op | source)
XLA Modules:
  0.0 205.9 jit_solution(2156913806340199756)
XLA Ops:
  0.6 0.8 copy.16.owners
  1.4 0.8 copy.17.slots
  2.1 0.0 copy-start
  2.1 3.1 %copy-done = bf16[32,128,896]{2,1,0:T(8,128)(2,1)S(1)} copy-done((bf16[32,128,896]{2,1,0:T(8,128)(2,1)S(1)}, bf16[32,128,896]{2,1,0:T(8,128)(2,1)}, u32[]{:S(2)}) %copy-start) | copy-done | bytes 7340056
  5.2 45.4 %fetch.1 = (bf16[16,128,896]{2,1,0:T(8,128)(2,1)S(1)}, s32[16,1,128]{2,1,0:T(1,128)S(1)}, s32[16,1,128]{2,1,0:T(1,128)S(1)}) custom-call(s32[8,2]{1,0:T(8,128)S(1)} %copy.16.owners, s32[8,2]{1,0:T(8,128)S(1)} %copy.17.slots, bf16[32,128,896]{2,1,0:T(8,128)(2,1)S(1)} %copy-done), custom_call_target="tpu_custom_call" | custom-call | tf_op jit(solution)/shard_map/fetch/pallas_call | solution.py:583
  50.7 0.0 copy-start.1
  50.7 1.8 copy-done.1
  52.5 0.1 eq.15
  52.6 71.9 %block.1 = (bf16[512,1024]{1,0:T(8,128)(2,1)}, bf16[512,1024]{1,0:T(8,128)(2,1)}, bf16[896,1024]{1,0:T(8,128)(2,1)}, bf16[896,1024]{1,0:T(8,128)(2,1)}, bf16[8,16,16,896]{3,2,1,0:T(8,128)(2,1)}) custom-call(bf16[2048,896]{1,0:T(8,128)(2,1)} %bitcast.6, bf16[512,1024]{1,0:T(8,128)(2,1)} %queries.1, bf16[512,1024]{1,0:T(8,128)(2,1)} %cotangent.1, ...), custom_call_target="tpu_custom_call" | custom-call | flops 22548578304 | bytes 25165824 | tf_op jit(solution)/shard_map/block/pallas_call | solution.py:98
  124.5 75.3 %send_back.1 = (bf16[896,1024]{1,0:T(8,128)(2,1)S(1)}, bf16[896,1024]{1,0:T(8,128)(2,1)S(1)}, bf16[16,3,16,896]{3,2,1,0:T(8,128)(2,1)S(1)}) custom-call(s32[16,1,128]{2,1,0:T(1,128)S(1)} %get-tuple-element.19.user, bf16[896,1024]{1,0:T(8,128)(2,1)} %get-tuple-element.20.part_key, bf16[896,1024]{1,0:T(8,128)(2,1)} %get-tuple-element.21.part_value, ...), custom_call_target="tpu_custom_call" | custom-call | tf_op jit(solution)/shard_map/send_back/pallas_call | solution.py:426
  199.8 0.4 convolution_convert_fusion
  200.2 1.2 copy.19
  201.4 2.3 %convert_element_type.10 = f32[896,1024]{1,0:T(8,128)} convert(bf16[896,1024]{1,0:T(8,128)(2,1)S(1)} %get-tuple-element.23) | non-fusion elementwise | flops 917504 | bytes 5505024 | tf_op jit(solution)/shard_map/convert_element_type | solution.py:623
  203.7 2.3 %convert_element_type.11 = f32[896,1024]{1,0:T(8,128)} convert(bf16[896,1024]{1,0:T(8,128)(2,1)S(1)} %get-tuple-element.24) | non-fusion elementwise | flops 917504 | bytes 5505024 | tf_op jit(solution)/shard_map/convert_element_type | solution.py:623
  (1 shorter events, 0.0 us)
Async XLA Ops:
  2.1 3.1 %copy-start = (bf16[32,128,896]{2,1,0:T(8,128)(2,1)S(1)}, bf16[32,128,896]{2,1,0:T(8,128)(2,1)}, u32[]{:S(2)}) copy-start(bf16[32,128,896]{2,1,0:T(8,128)(2,1)} %database.1) | copy-start | bytes 22020100
  50.7 1.8 copy-start.1

commit v4 on v1

v4 whole, which is shorter than its diff:
```python
import functools

import jax
import jax.numpy as jnp
from jax import lax
from jax.experimental import pallas as pl
from jax.experimental.pallas import tpu as pltpu
from jax.sharding import PartitionSpec as P

HD = 128
SPAN = 64
CAP = 3
PARTS = 2
GPARTS = 2
NT = (((1,), (1,)), ((), ()))
TN = (((0,), (0,)), ((), ()))
F32 = jnp.float32
BF16 = jnp.bfloat16


def dot(a, b):
    return jnp.dot(a, b, preferred_element_type=F32)


MESH = pl.DeviceIdType.MESH


class Links:
    def __init__(self, side_z, side_y, side_x):
        db, rack = lax.axis_index("db"), lax.axis_index("rack")
        self.db, self.rack = db, rack
        self.z, self.y = db // side_y, db % side_y
        self.x, self.core = rack // 2, rack % 2
        self.side_x = side_x
        self.ids = {
            ("y", 1): (self.z * side_y + (self.y + 1) % side_y, rack),
            ("y", -1): (self.z * side_y + (self.y + side_y - 1) % side_y, rack),
            ("z", 1): ((self.z + 1) % side_z * side_y + self.y, rack),
            ("z", -1): ((self.z + side_z - 1) % side_z * side_y + self.y, rack),
            ("x", 1): (db, (self.x + 1) % side_x * 2 + self.core),
            ("x", -1): (db, (self.x + side_x - 1) % side_x * 2 + self.core),
            ("core", 1): (db, self.x * 2 + 1 - self.core),
        }

    def place(self, axis):
        return {"y": self.y, "z": self.z, "x": self.x}[axis]


class Mail:
    def __init__(self, send_sems, recv_sems):
        self.send_sems, self.recv_sems, self.book = send_sems, recv_sems, {}

    def plan(self, name, source, target, device):
        self.book[name] = (len(self.book), source, target, device)

    def copy(self, name):
        n, source, target, device = self.book[name]
        return pltpu.make_async_remote_copy(
            src_ref=source(), dst_ref=target(), send_sem=self.send_sems.at[n], recv_sem=self.recv_sems.at[n], device_id=device,
            device_id_type=MESH,
        )

    def start(self, *names):
        for name in names:
            self.copy(name).start()

    def arrive(self, *names):
        for name in names:
            self.copy(name).wait_recv()

    def settle(self):
        for name in self.book:
            self.copy(name).wait_send()


def greet(links, peers):
    barrier = pltpu.get_barrier_semaphore()
    others = [links.ids[("core", 1)], links.ids[("x", 1)], links.ids[("x", -1)]]
    for device in others:
        pl.semaphore_signal(barrier, inc=1, device_id=device, device_id_type=MESH)

    @pl.loop(1, peers)
    def _(far):
        pl.semaphore_signal(barrier, inc=1, device_id=((links.db + far) % peers, links.rack), device_id_type=MESH)

    return len(others) + peers - 1


def add(*terms):
    total = terms[0].astype(F32)
    for term in terms[1:]:
        total = total + term.astype(F32)
    return total.astype(BF16)


class Reduction:
    def __init__(self, tag, links, mail, part, full, first_column, columns, axes, near, far, middle):
        self.tag, self.links, self.mail = tag, links, mail
        self.part, self.full, self.first_column, self.columns = part, full, first_column, columns
        self.near, self.far, self.middle = near, far, middle
        self.rows = part.shape[0] // 4
        self.places = [links.place(axis) for axis in axes]
        self.across = columns // 128
        self.short = self.rows * self.across // 4
        self.sides = [(0, self.rows // 32 * 16), (self.rows // 32 * 16, self.rows - self.rows // 32 * 16)]
        whole = (self.short + 31) // 32 * 16
        self.bits = [(0, whole), (whole, self.short - whole)]
        up = [links.ids[(axis, 1)] for axis in axes]
        down = [links.ids[(axis, -1)] for axis in axes]
        one, two = self.places
        for level, at, buffer, sides, me, k in (("n", self.wide, near, self.sides, one, 0), ("f", self.small, far, self.bits, two, 1)):
            lot = lambda ref, slot, side, sides=sides: (lambda: ref.at[slot, pl.ds(0, sides[side][1])])
            spot = lambda far_off, side, at=at, me=me: (lambda: at((me + far_off) % 4, side))
            self.plan(level + "ra", spot(2, 0), lot(buffer, 0, 0), up[k])
            self.plan(level + "rb", spot(2, 1), lot(buffer, 1, 1), down[k])
            self.plan(level + "db", spot(1, 1), lot(buffer, 3, 1), up[k])
            self.plan(level + "da", spot(3, 0), lot(buffer, 2, 0), down[k])
            self.plan(level + "sa", lot(buffer, 0, 0), lot(buffer, 4, 0), up[k])
            self.plan(level + "sb", lot(buffer, 1, 1), lot(buffer, 5, 1), down[k])
        for level, at, sides, size, me, k in (("g", self.piece, self.bits, self.short, two, 1), ("h", self.band, self.sides, self.rows, one, 0)):
            spot = lambda far_off, first, size, at=at, me=me: (lambda: at((me + far_off) % 4, first, size))
            for name, far_off, (first, length), device in (
                ("up", 0, (0, size), up[k]), ("down", 0, (0, size), down[k]), ("on", 3, sides[0], up[k]), ("back", 1, sides[1], down[k]),
            ):
                self.plan(level + name, spot(far_off, first, length), spot(far_off, first, length), device)

    def plan(self, name, source, target, device):
        self.mail.plan((self.tag, name), source, target, device)

    def start(self, *names):
        self.mail.start(*[(self.tag, name) for name in names])

    def arrive(self, *names):
        self.mail.arrive(*[(self.tag, name) for name in names])

    def wide(self, one, side):
        first, size = self.sides[side]
        return self.part.at[pl.ds(pl.multiple_of(one * self.rows + first, 16), size), pl.ds(self.first_column, self.columns)]

    def small(self, two, side):
        first, size = self.bits[side]
        return self.middle.at[
            pl.ds(pl.multiple_of(two // self.across * self.short + first, 16), size),
            pl.ds(pl.multiple_of(two % self.across * 128, 128), 128),
        ]

    def piece(self, two, first, size):
        row = self.places[0] * self.rows + two // self.across * self.short + first
        column = self.first_column + two % self.across * 128
        return self.full.at[pl.ds(pl.multiple_of(row, 16), size), pl.ds(pl.multiple_of(column, 128), 128)]

    def band(self, one, first, size):
        return self.full.at[pl.ds(pl.multiple_of(one * self.rows + first, 16), size), pl.ds(self.first_column, self.columns)]

    def join(self, level, at, buffer, sides, me):
        for side, letter, far_off in ((0, "a", 1), (1, "b", 3)):
            size = sides[side][1]
            self.arrive(level + "r" + letter)
            buffer[side, :size] = add(buffer[side, :size], at((me + far_off) % 4, side)[...])
            self.start(level + "s" + letter)

    def total(self, level, at, buffer, sides, me, side):
        letter, size = "ab"[side], sides[side][1]
        self.arrive(level + "d" + letter, level + "s" + letter)
        return add(buffer[2 + side, :size], buffer[4 + side, :size], at(me, side)[...])

    def stage(self, number):
        one, two = self.places
        if number == 0:
            self.start("nra", "nrb", "ndb", "nda")
        elif number == 1:
            self.join("n", self.wide, self.near, self.sides, one)
        elif number == 2:
            for side, (first, size) in enumerate(self.sides):
                self.middle[first:first + size, :] = self.total("n", self.wide, self.near, self.sides, one, side)
            self.start("fra", "frb", "fdb", "fda")
        elif number == 3:
            self.join("f", self.small, self.far, self.bits, two)
        elif number == 4:
            for side, (first, size) in enumerate(self.bits):
                self.piece(two, first, size)[...] = self.total("f", self.small, self.far, self.bits, two, side)
            self.start("gup", "gdown")
        elif number == 6:
            self.arrive("gon", "gback")
            self.start("hup", "hdown")
        elif number == 8:
            self.arrive("hon", "hback")
        else:
            level = "g" if number == 5 else "h"
            self.arrive(level + "up")
            self.start(level + "on")
            self.arrive(level + "down")
            self.start(level + "back")


class Return:
    def __init__(self, links, mail, use_grad, user, returned, crossed, ring, mine, leaving, leave_sems, land_sems):
        self.links, self.mail, self.use_grad, self.user, self.returned = links, mail, use_grad, user, returned
        self.crossed, self.ring, self.mine, self.leaving = crossed, ring, mine, leaving
        self.leave_sems, self.land_sems = leave_sems, land_sems
        self.half = mine.shape[0] // 2
        up, down, across = links.ids[("x", 1)], links.ids[("x", -1)], links.ids[("core", 1)]
        for side in (0, 1):
            for far_off in (2, 1, 3, 0):
                mail.plan(("c", far_off, side), self.partner(far_off, side), self.spot(far_off, side), across)
        slot = lambda n: (lambda: ring.at[n])
        mail.plan("xra", self.spot(2, 0), slot(0), up)
        mail.plan("xda", self.spot(3, 0), slot(2), down)
        mail.plan("xrb", self.spot(2, 1), slot(1), down)
        mail.plan("xdb", self.spot(1, 1), slot(3), up)
        mail.plan("xsa", slot(0), slot(4), up)
        mail.plan("xsb", slot(1), slot(5), down)

    def uses(self, side):
        return pl.ds(side * self.half, self.half)

    def spot(self, far_off, side):
        return lambda: self.crossed.at[(self.links.x + far_off) % 4, self.uses(side)]

    def partner(self, far_off, side):
        return lambda: self.use_grad.at[(self.links.x + far_off) % 4 * 2 + 1 - self.links.core, self.uses(side)]

    def cross(self, side):
        self.mail.start(*[("c", far_off, side) for far_off in (2, 1, 3, 0)])

    def ring_out(self, side):
        links, mail, half = self.links, self.mail, self.half
        first, second = (("xra", 2), ("xda", 3)) if side == 0 else (("xrb", 2), ("xdb", 1))
        for name, far_off in (first, second, (None, 1 if side == 0 else 3), (None, 0)):
            x = (links.x + far_off) % 4
            mail.arrive(("c", far_off, side))

            @pl.loop(side * half, (side + 1) * half)
            def _(n):
                self.crossed[x, n] = add(self.crossed[x, n], self.use_grad[x * 2 + links.core, n])

            if name:
                mail.start(name)

    def ring_on(self, side):
        letter, far_off = ("a", 1) if side == 0 else ("b", 3)
        self.mail.arrive("xr" + letter)
        own = self.spot(far_off, side)()

        @pl.loop(0, self.half)
        def _(n):
            self.ring[side, n] = add(self.ring[side, n], own[n])

        self.mail.start("xs" + letter)

    def ring_end(self, side):
        letter = "ab"[side]
        self.mail.arrive("xd" + letter, "xs" + letter)
        own = self.spot(0, side)()

        @pl.loop(0, self.half)
        def _(n):
            self.mine[side * self.half + n] = add(self.ring[2 + side, n], self.ring[4 + side, n], own[n])

    def post(self):
        links, peers = self.links, self.returned.shape[0]
        self.mine[2 * self.half] = jnp.zeros(self.mine.shape[1:], BF16)

        def fill(peer, target):
            for k in range(CAP):
                target[peer, k] = self.mine[self.user[peer, 0, k]]

        @pl.loop(1, peers)
        def _(far_off):
            fill((links.db + far_off) % peers, self.leaving)
            self.copy(far_off).start()

        fill(links.db, self.returned)

    def received(self):
        pl.loop(1, self.returned.shape[0])(lambda far_off: self.copy(far_off).wait())

    def copy(self, far_off):
        links = self.links
        peer = (links.db + far_off) % self.returned.shape[0]
        return pltpu.make_async_remote_copy(
            src_ref=self.leaving.at[peer], dst_ref=self.returned.at[links.db], send_sem=self.leave_sems.at[far_off],
            recv_sem=self.land_sems.at[far_off], device_id=(peer, links.rack), device_id_type=MESH,
        )


def block_step(step, spans, heads, panels, queries, cotangent, w_key, w_value, attended, grad_queries, part_key, part_value,
               use_grad, flipped, rows_kv, grads_kv, left, right, pair, stacked, wide):
    keys = panels.shape[0] // spans
    width = panels.shape[1]
    scale = HD ** -0.5

    @pl.when(step == 0)
    def _():
        left[...] = jnp.zeros_like(left)
        right[...] = jnp.zeros_like(right)
        for c in range(spans):
            flipped[:, c * keys:(c + 1) * keys] = panels[c * keys:(c + 1) * keys, :].T

    @pl.when(step < heads)
    def _():
        columns = pl.ds(pl.multiple_of(step * HD, HD), HD)
        wide[:, :HD] = w_key[:, columns]
        wide[:, HD:] = w_value[:, columns]

        @pl.loop(0, PARTS)
        def _(n):
            size = panels.shape[0] // PARTS
            at = pl.ds(pl.multiple_of(n * size, size), size)
            rows_kv[at, :] = dot(panels[at, :], wide[...]).astype(BF16)

        for c in range(spans):
            tokens = slice(c * SPAN, (c + 1) * SPAN)
            query, grad = queries[tokens, :], cotangent[tokens, :]
            left[c, :SPAN, :HD] = query
            left[c, SPAN:, HD:] = grad
            right[c, :SPAN, HD:] = grad
            right[c, SPAN:, :HD] = query
        for c in range(spans):
            pair[c] = lax.dot_general(left[c], rows_kv[c * keys:(c + 1) * keys, :], NT, preferred_element_type=F32)
        for c in range(spans):
            scores = pair[c, :SPAN] * scale
            raised = jnp.exp(scores - jnp.max(scores, axis=-1, keepdims=True))
            probs = raised * (1.0 / jnp.sum(raised, axis=-1, keepdims=True))
            stacked[c, :SPAN] = probs.astype(BF16)
            grad_probs = pair[c, SPAN:]
            delta = jnp.sum(probs * grad_probs, axis=-1, keepdims=True)
            stacked[c, SPAN:] = (probs * (grad_probs - delta) * scale).astype(BF16)
        for c in range(spans):
            tokens = slice(c * SPAN, (c + 1) * SPAN)
            own = slice(c * keys, (c + 1) * keys)
            out = dot(stacked[c], rows_kv[own, :])
            attended[tokens, :] = out[:SPAN, HD:].astype(BF16)
            grad_queries[tokens, :] = out[SPAN:, :HD].astype(BF16)
        for c in range(spans):
            own = slice(c * keys, (c + 1) * keys)
            grads_kv[step, own, :] = lax.dot_general(stacked[c], right[c], TN, preferred_element_type=F32).astype(BF16)

        @pl.loop(0, GPARTS)
        def _(n):
            size = width // GPARTS
            at = pl.ds(pl.multiple_of(n * size, size), size)
            total = dot(flipped[at, :], grads_kv[step]).astype(BF16)
            part_key[at, columns] = total[:, :HD]
            part_value[at, columns] = total[:, HD:]

    @pl.when(step >= heads)
    def _():
        c = step - heads
        own = pl.ds(pl.multiple_of(c * keys, keys), keys)
        total = jnp.zeros((keys, width), F32)
        for h in range(heads):
            columns = slice(h * HD, (h + 1) * HD)
            weights = jnp.concatenate([w_key[:, columns], w_value[:, columns]], axis=1)
            total = total + lax.dot_general(grads_kv[h, own, :], weights, NT, preferred_element_type=F32)
        total = total.astype(BF16)
        pieces, uses, rows = use_grad.shape[0], use_grad.shape[1] // spans, use_grad.shape[2]
        for n in range(uses):
            for r in range(pieces):
                first = (n * pieces + r) * rows
                use_grad[r, c * uses + n, :, :] = total[first:first + rows, :]


GROUPS = 4


def block_kernel(spans, heads, user, panels, queries, cotangent, w_key, w_value, attended, grad_queries, out_key, out_value,
                 out_returned, full_key, full_value, returned, flipped, rows_kv, grads_kv, left, right, pair, stacked, wide, part_key, part_value, use_grad, near, far,
                 middle, crossed, ring, mine, leaving, send_sems, recv_sems, leave_sems, land_sems, out_sems):
    step = pl.program_id(0)
    links = Links(4, 4, 4)
    mail = Mail(send_sems, recv_sems)
    columns = part_key.shape[1] // GROUPS
    items = []
    for g in range(GROUPS):
        for m, (part, full, axes) in enumerate(((part_key, full_key, "yz"), (part_value, full_value, "zy"))):
            n = g * 2 + m
            items.append(Reduction(n, links, mail, part, full, g * columns, columns, axes, near.at[n], far.at[n], middle.at[n]))
    back = Return(links, mail, use_grad, user, returned, crossed, ring, mine, leaving, leave_sems, land_sems)

    def advance(*moves):
        for g, number in moves:
            items[2 * g].stage(number)
            items[2 * g + 1].stage(number)
            if number == 8:
                result(g, 0).start()
                result(g, 1).start()

    def result(g, m):
        source, target = ((full_key, out_key), (full_value, out_value))[m]
        at = (slice(None), pl.ds(g * columns, columns))
        return pltpu.make_async_copy(source.at[at], target.at[at], out_sems.at[2 * g + m])

    @pl.when(step == 0)
    def _():
        greet(links, returned.shape[0])

    block_step(step, spans, heads, panels, queries, cotangent, w_key, w_value, attended, grad_queries, part_key, part_value,
               use_grad, flipped, rows_kv, grads_kv, left, right, pair, stacked, wide)

    for after in range(1, heads):
        moves = [(g, after - 2 * g - 1) for g in reversed(range(GROUPS)) if 0 <= after - 2 * g - 1 <= 8]

        @pl.when(step == after)
        def _():
            if after == 1:
                pl.semaphore_wait(pltpu.get_barrier_semaphore(), 3 + returned.shape[0] - 1)
            advance(*moves)

    @pl.when(step == heads + spans // 2 - 1)
    def _():
        back.cross(0)
        advance((3, 1), (2, 3), (1, 5), (0, 7))

    @pl.when(step == heads + spans - 1)
    def _():
        back.cross(1)
        back.ring_out(0)
        advance((3, 2), (2, 4), (1, 6), (0, 8))
        back.ring_out(1)
        back.ring_on(0)
        back.ring_on(1)
        advance((3, 3), (2, 5), (1, 7))
        back.ring_end(0)
        back.ring_end(1)
        back.post()
        advance((3, 4), (2, 6), (1, 8), (3, 5), (2, 7), (3, 6), (2, 8), (3, 7), (3, 8))
        back.received()
        last = pltpu.make_async_copy(returned, out_returned, out_sems.at[2 * GROUPS])
        last.start()
        mail.settle()
        for g in range(GROUPS):
            result(g, 0).wait()
            result(g, 1).wait()
        last.wait()


def block_call(user, panels, queries, cotangent, w_key, w_value, racks, peers):
    uses, panel_len, width = panels.shape
    spans = queries.shape[0] // SPAN
    features = w_key.shape[1]
    heads = features // HD
    rows = panel_len // racks
    total = uses * panel_len
    columns = features // GROUPS
    messages = 2 * GROUPS * 20 + 14
    by_head = lambda size: pl.BlockSpec((size, HD), lambda i: (0, jnp.minimum(i, heads - 1)))
    whole = lambda a, b: pl.BlockSpec((a, b), lambda i: (0, 0), pipeline_mode=pl.Buffered(1))
    anywhere = pl.BlockSpec(memory_space=pl.ANY)
    return pl.pallas_call(
        functools.partial(block_kernel, spans, heads),
        grid=(heads + spans,),
        out_shape=(
            jax.ShapeDtypeStruct(queries.shape, BF16),
            jax.ShapeDtypeStruct(queries.shape, BF16),
            jax.ShapeDtypeStruct((width, features), BF16),
            jax.ShapeDtypeStruct((width, features), BF16),
            jax.ShapeDtypeStruct((peers, CAP, rows, width), BF16),
        ),
        in_specs=[
            pl.BlockSpec(memory_space=pltpu.SMEM), whole(total, width), by_head(queries.shape[0]), by_head(queries.shape[0]),
            whole(width, features), whole(width, features),
        ],
        out_specs=[by_head(queries.shape[0]), by_head(queries.shape[0]), anywhere, anywhere, anywhere],
        scratch_shapes=[
            pltpu.VMEM((width, features), BF16),
            pltpu.VMEM((width, features), BF16),
            pltpu.VMEM((peers, CAP, rows, width), BF16),
            pltpu.VMEM((width, total), BF16),
            pltpu.VMEM((total, 2 * HD), BF16),
            pltpu.VMEM((heads, total, 2 * HD), BF16),
            pltpu.VMEM((spans, 2 * SPAN, 2 * HD), BF16),
            pltpu.VMEM((spans, 2 * SPAN, 2 * HD), BF16),
            pltpu.VMEM((spans, 2 * SPAN, total // spans), F32),
            pltpu.VMEM((spans, 2 * SPAN, total // spans), BF16),
            pltpu.VMEM((width, 2 * HD), BF16),
            pltpu.VMEM((width, features), BF16),
            pltpu.VMEM((width, features), BF16),
            pltpu.VMEM((racks, uses, rows, width), BF16),
            pltpu.VMEM((2 * GROUPS, 6, width // 8, columns), BF16),
            pltpu.VMEM((2 * GROUPS, 6, 64, 128), BF16),
            pltpu.VMEM((2 * GROUPS, width // 4, columns), BF16),
            pltpu.VMEM((4, uses, rows, width), BF16),
            pltpu.VMEM((6, uses // 2, rows, width), BF16),
            pltpu.VMEM((uses + 1, rows, width), BF16),
            pltpu.VMEM((peers, CAP, rows, width), BF16),
            pltpu.SemaphoreType.DMA((messages,)),
            pltpu.SemaphoreType.DMA((messages,)),
            pltpu.SemaphoreType.DMA((peers,)),
            pltpu.SemaphoreType.DMA((peers,)),
            pltpu.SemaphoreType.DMA((2 * GROUPS + 1,)),
        ],
        compiler_params=pltpu.CompilerParams(
            collective_id=1, has_side_effects=True, vmem_limit_bytes=58 * 1024 * 1024
        ),
        name="block",
    )(user, panels.reshape(total, width), queries, cotangent, w_key, w_value)


def fetch_kernel(cuts, owners, slots, database, panels, asked, user, stored, wanted, heard, leaving, landing, mine, load_sem, ask_send,
                 ask_recv, leave_sems, land_sems, own_sems, send_sems, recv_sems):
    links = Links(4, 4, 4)
    peers = asked.shape[0]
    local_rows, _, width = stored.shape
    uses, rows = mine.shape[0], mine.shape[1]
    nbrs = owners.shape[1]
    my_rows = lambda x, core: pl.ds(pl.multiple_of((x * 2 + core) * rows, rows), rows)
    load = pltpu.make_async_copy(database.at[:, my_rows(links.x, links.core), :], stored, load_sem.at[0])
    load.start()
    signals = greet(links, peers)
    pl.semaphore_wait(pltpu.get_barrier_semaphore(), signals)

    peer_of = lax.broadcasted_iota(jnp.int32, (peers, 1, 128), 0)
    lane = lax.broadcasted_iota(jnp.int32, (peers, 1, 128), 2)
    seen = jnp.zeros((peers, 1, 128), jnp.int32)
    rows_wanted = jnp.full((peers, 1, 128), local_rows, jnp.int32)
    users = jnp.full((peers, 1, 128), uses, jnp.int32)
    for u in range(uses):
        named = peer_of == owners[u // nbrs, u % nbrs]
        here = named & (lane == seen)
        rows_wanted = jnp.where(here, slots[u // nbrs, u % nbrs], rows_wanted)
        users = jnp.where(here, u, users)
        seen = seen + named.astype(jnp.int32)
    wanted[...] = rows_wanted
    user[...] = users

    def ask(far):
        peer = (links.db + far) % peers
        return pltpu.make_async_remote_copy(
            src_ref=wanted.at[peer], dst_ref=asked.at[links.db], send_sem=ask_send.at[far], recv_sem=ask_recv.at[far],
            device_id=(peer, links.rack), device_id_type=MESH,
        )

    pl.loop(1, peers)(lambda far: ask(far).start())
    asked[links.db] = wanted[links.db]
    load.wait()
    pl.loop(1, peers)(lambda far: ask(far).wait())
    tables = pltpu.make_async_copy(asked, heard, load_sem.at[1])
    tables.start()
    tables.wait()

    def answer(c, far):
        peer = (links.db + far) % peers
        return pltpu.make_async_remote_copy(
            src_ref=leaving[c].at[peer], dst_ref=landing[c].at[links.db], send_sem=leave_sems.at[c, far],
            recv_sem=land_sems.at[c, far], device_id=(peer, links.rack), device_id_type=MESH,
        )

    def fill(c, peer, target):
        for k in range(CAP):
            row = jnp.minimum(heard[peer, 0, k], local_rows - 1)
            target[peer, k] = stored[row, :, cuts[c]:cuts[c + 1]]

    for c in range(len(cuts) - 1):
        @pl.loop(1, peers)
        def _(far):
            fill(c, (links.db + far) % peers, leaving[c])
            answer(c, far).start()

        fill(c, links.db, landing[c])

    mail = Mail(send_sems, recv_sems)
    up, down, across = links.ids[("x", 1)], links.ids[("x", -1)], links.ids[("core", 1)]
    own_copies = []
    half = uses // 2

    def out(c, far, first, size):
        return panels.at[pl.ds(first, size), my_rows((links.x + far) % 4, links.core), pl.ds(cuts[c], cuts[c + 1] - cuts[c])]

    def pass_on(name, c, far, first, size, device):
        spot = lambda: out(c, far, first, size)
        mail.plan((name, c), spot, spot, device)
        mail.start((name, c))

    def exchange(c):
        mail.arrive(("up", c))
        pass_on("on", c, 3, 0, half, up)
        pass_on("cross3", c, 3, 0, uses, across)
        mail.arrive(("down", c))
        pass_on("back", c, 1, half, half, down)
        pass_on("cross1", c, 1, 0, uses, across)

    def finish(c):
        mail.arrive(("on", c))
        pass_on("cross2a", c, 2, 0, half, across)
        mail.arrive(("back", c))
        pass_on("cross2b", c, 2, half, half, across)

    count = len(cuts) - 1
    for c in range(count):
        pl.loop(1, peers)(lambda far: answer(c, far).wait())
        for u in range(uses):
            owner = owners[u // nbrs, u % nbrs]
            rank = jnp.int32(0)
            for v in range(u):
                rank = rank + (owners[v // nbrs, v % nbrs] == owner).astype(jnp.int32)
            mine[u, :, cuts[c]:cuts[c + 1]] = landing[c][owner, jnp.minimum(rank, CAP - 1)]
        source = mine.at[:, :, pl.ds(cuts[c], cuts[c + 1] - cuts[c])]
        target = out(c, 0, 0, uses)
        for name, device in (("up", up), ("down", down), ("cross0", across)):
            mail.plan((name, c), lambda source=source: source, lambda target=target: target, device)
            mail.start((name, c))
        copy = pltpu.make_async_copy(source, target, own_sems.at[c])
        copy.start()
        own_copies.append(copy)
        if c > 0:
            exchange(c - 1)
    exchange(count - 1)
    for c in range(count):
        finish(c)
    for c in range(count):
        mail.arrive(("cross0", c), ("cross1", c), ("cross3", c), ("cross2a", c), ("cross2b", c))
    for copy in own_copies:
        copy.wait()
    mail.settle()


CUTS = (0, 512, 896)


def fetch_call(owners, slots, database, peers, racks):
    uses = owners.shape[0] * owners.shape[1]
    local_rows, panel_len, width = database.shape
    rows = panel_len // racks
    parts = len(CUTS) - 1
    chunk = lambda c: pltpu.VMEM((peers, CAP, rows, CUTS[c + 1] - CUTS[c]), BF16)
    vmem = pl.BlockSpec(memory_space=pltpu.VMEM)
    smem = pl.BlockSpec(memory_space=pltpu.SMEM)
    anywhere = pl.BlockSpec(memory_space=pl.ANY)
    sems = pltpu.SemaphoreType.DMA
    return pl.pallas_call(
        functools.partial(fetch_kernel, CUTS),
        out_shape=(
            jax.ShapeDtypeStruct((uses, panel_len, width), BF16),
            jax.ShapeDtypeStruct((peers, 1, 128), jnp.int32),
            jax.ShapeDtypeStruct((peers, 1, 128), jnp.int32),
        ),
        in_specs=[smem, smem, anywhere],
        out_specs=(anywhere, vmem, vmem),
        scratch_shapes=[
            pltpu.VMEM((local_rows, rows, width), BF16),
            pltpu.VMEM((peers, 1, 128), jnp.int32),
            pltpu.SMEM((peers, 1, 128), jnp.int32),
            [chunk(c) for c in range(parts)],
            [chunk(c) for c in range(parts)],
            pltpu.VMEM((uses, rows, width), BF16),
            sems((2,)), sems((peers,)), sems((peers,)), sems((parts, peers)), sems((parts, peers)), sems((parts,)),
            sems((9 * parts,)), sems((9 * parts,)),
        ],
        compiler_params=pltpu.CompilerParams(
            collective_id=0, has_side_effects=True, vmem_limit_bytes=24 * 1024 * 1024
        ),
        name="fetch",
    )(owners, slots, database)


def pick(selector, source):
    return jnp.einsum("ns,spw->npw", selector, source, preferred_element_type=F32).astype(BF16)


def local(queries, cotangent, database, w_key, w_value, neighbour_owner, neighbour_slot):
    peer_count = lax.axis_size("db")
    racks = lax.axis_size("rack")
    local_rows, _, width = database.shape
    rows = database.shape[1] // racks
    panels, asked, user = fetch_call(neighbour_owner, neighbour_slot, database, peer_count, racks)
    asked_rows = asked[:, 0, :CAP].reshape(peer_count * CAP)
    selector = (asked_rows[:, None] == jnp.arange(local_rows, dtype=jnp.int32)[None, :]).astype(BF16)
    attended, grad_query, full_key, full_value, returned = block_call(
        user, panels, queries, cotangent, w_key, w_value, racks, peer_count
    )
    grad_w_key, grad_w_value = full_key.astype(F32), full_value.astype(F32)
    grad_database = pick(selector.T, returned.reshape(peer_count * CAP, rows, width))
    return attended, grad_query, grad_w_key, grad_w_value, grad_database


def solution(mesh):
    return jax.shard_map(
        local,
        mesh=mesh,
        in_specs=(
            P("db", "rack"), P("db", "rack"), P("db", None, None), P(None, "rack"), P(None, "rack"), P("db", None), P("db", None),
        ),
        out_specs=(P("db", "rack"), P("db", "rack"), P(None, "rack"), P(None, "rack"), P("db", "rack", None)),
        check_vma=False,
    )
```

time: 322 us -> 171 us (0.53)
  waiting for transfers between devices: 175 us -> 0 us
  Pallas kernels: 71.9 us -> 153 us
  blocking collectives: 22.6 us -> 0 us
  starting transfers between devices: 15.2 us -> 0 us
  between operations: 13.8 us -> 0.69 us
  other arithmetic: 7.77 us -> 4.5 us
    psum x1 -> x0, waiting for transfers between devices: 104 us -> none  [local(): grad_w_key = lax.psum(part_key, 'db').astype(F32)]
    pallas_call x0 -> x1, Pallas kernels: none -> 45.4 us  [fetch_call(): pl.pallas_call(functools.partial(fetch_kernel, CUTS), out_shape=(jax.Shap...]
    reduce_scatter x1 -> x0, waiting for transfers between devices: 36.1 us -> none  [local(): lax.psum_scatter(use_grad, 'rack', scatter_dimension=0, tiled=True)[0]]
    pallas_call x1, Pallas kernels: 71.9 us -> 107 us  [block_call(): pl.pallas_call(functools.partial(block_kernel, spans, heads), grid=(heads...]
    all_gather x1 -> x0, waiting for transfers between devices: 27.4 us -> none  [local(): panels = lax.all_gather(mine, 'rack', axis=1, tiled=True)]
    all_to_all x1 -> x0, blocking collectives: 22.6 us -> none  [local(): lax.all_to_all(answer, 'db', split_axis=0, concat_axis=0, tiled=True)]
    all_to_all x2 -> x0, starting transfers between devices: 15.1 us -> none  [the longest x1 8.13 us: local(): lax.all_to_all(wanted.reshape(peer_count, CAP), 'db', split_axis=0, conca...]
    unnamed x4 -> x19, local copies, waits for them, and re-layouts: 1.96 us -> 10.8 us
  transfers between devices with their start and end apart: 5 -> 0, of which waited for: 4 -> 0; matrix products, arithmetic and copies ran while one was open for 3% -> 0% of each run, Pallas kernels for 0% -> 0%
where the time goes in v4:
time: 171 us
  Pallas kernels  153 us (89%)
  local copies, waits for them, and re-layouts  10.9 us (6%)
  other arithmetic  4.5 us (3%)
  matrix products  1.86 us (1%)
    pallas_call x1, Pallas kernels, block_call(): pl.pallas_call(functools.partial(block_kernel, spans, heads), grid=(heads...  107 us
    pallas_call x1, Pallas kernels, fetch_call(): pl.pallas_call(functools.partial(fetch_kernel, CUTS), out_shape=(jax.Shap...  45.4 us
    unnamed x19, local copies, waits for them, and re-layouts  10.8 us
    convert_element_type x2, other arithmetic, local(): grad_w_key, grad_w_value = (full_key.astype(F32), full_value.astype(F32))  4.5 us

profile of v4, /device:TPU:0, one launch (start us, length us, event | category | flops | bytes accessed | tf_op | source)
XLA Modules:
  0.0 170.7 jit_solution(8771360709166317120)
XLA Ops:
  0.6 0.8 copy.16.owners
  1.4 0.8 copy.17.slots
  2.1 0.0 copy-start
  2.1 3.1 %copy-done = bf16[32,128,896]{2,1,0:T(8,128)(2,1)S(1)} copy-done((bf16[32,128,896]{2,1,0:T(8,128)(2,1)S(1)}, bf16[32,128,896]{2,1,0:T(8,128)(2,1)}, u32[]{:S(2)}) %copy-start) | copy-done | bytes 7340056
  5.2 45.4 %fetch.1 = (bf16[16,128,896]{2,1,0:T(8,128)(2,1)S(1)}, s32[16,1,128]{2,1,0:T(1,128)S(1)}, s32[16,1,128]{2,1,0:T(1,128)S(1)}) custom-call(s32[8,2]{1,0:T(8,128)S(1)} %copy.16.owners, s32[8,2]{1,0:T(8,128)S(1)} %copy.17.slots, bf16[32,128,896]{2,1,0:T(8,128)(2,1)S(1)} %copy-done), custom_call_target="tpu_custom_call" | custom-call | tf_op jit(solution)/shard_map/fetch/pallas_call | solution.py:631
  50.6 0.0 copy-start.1
  50.6 1.8 %copy-done.1 = bf16[16,128,896]{2,1,0:T(8,128)(2,1)} copy-done((bf16[16,128,896]{2,1,0:T(8,128)(2,1)}, bf16[16,128,896]{2,1,0:T(8,128)(2,1)S(1)}, u32[]{:S(2)}) %copy-start.1) | copy-done | bytes 3670040
  52.5 0.0 copy-start.2
  52.5 0.6 copy-done.2
  53.1 0.1 eq.15
  53.2 107.3 %block.1 = (bf16[512,1024]{1,0:T(8,128)(2,1)}, bf16[512,1024]{1,0:T(8,128)(2,1)}, bf16[896,1024]{1,0:T(8,128)(2,1)}, bf16[896,1024]{1,0:T(8,128)(2,1)}, bf16[16,3,16,896]{3,2,1,0:T(8,128)(2,1)}) custom-call(s32[16,1,128]{2,1,0:T(1,128)} %copy-done.2, bf16[2048,896]{1,0:T(8,128)(2,1)} %bitcast.5, bf16[512,1024]{1,0:T(8,128)(2,1)} %queries.1, ...), custom_call_target="tpu_custom_call" | custom-call | tf_op jit(solution)/shard_map/block/pallas_call | solution.py:450
  160.5 0.0 copy-start.4
  160.5 1.9 %convolution_convert_fusion = bf16[32,16,896]{2,0,1:T(8,128)(2,1)S(1)} fusion(bf16[48,16,896]{2,1,0:T(8,128)(2,1)} %bitcast.6, s32[48]{0:T(128)S(1)} %eq.15), kind=kOutput, calls=%fused_computation | convolution fusion | flops 44500480 | bytes 2293952 | tf_op jit(solution)/shard_map/ns,spw->npw/dot_general | solution.py:658
  162.4 1.2 copy.19
  163.6 0.0 copy-done.4
  163.6 0.0 copy-start.3
  163.6 2.3 %convert_element_type.10 = f32[896,1024]{1,0:T(8,128)} convert(bf16[896,1024]{1,0:T(8,128)(2,1)S(1)} %copy-done.4) | non-fusion elementwise | flops 917504 | bytes 5505024 | tf_op jit(solution)/shard_map/convert_element_type | solution.py:672
  165.8 0.0 copy-done.3
  165.9 0.0 copy-start.6
  165.9 2.3 %convert_element_type.11 = f32[896,1024]{1,0:T(8,128)} convert(bf16[896,1024]{1,0:T(8,128)(2,1)S(1)} %copy-done.3) | non-fusion elementwise | flops 917504 | bytes 5505024 | tf_op jit(solution)/shard_map/convert_element_type | solution.py:672
  168.1 0.0 copy-done.6
  168.1 1.0 copy.24
  169.1 0.6 copy-done.5
  169.7 1.0 copy.25
  (2 shorter events, 0.0 us)
Async XLA Ops:
  2.1 3.1 %copy-start = (bf16[32,128,896]{2,1,0:T(8,128)(2,1)S(1)}, bf16[32,128,896]{2,1,0:T(8,128)(2,1)}, u32[]{:S(2)}) copy-start(bf16[32,128,896]{2,1,0:T(8,128)(2,1)} %database.1) | copy-start | bytes 22020100
  50.6 1.8 %copy-start.1 = (bf16[16,128,896]{2,1,0:T(8,128)(2,1)}, bf16[16,128,896]{2,1,0:T(8,128)(2,1)S(1)}, u32[]{:S(2)}) copy-start(bf16[16,128,896]{2,1,0:T(8,128)(2,1)S(1)} %get-tuple-element.14) | copy-start | bytes 11010052
  52.5 0.6 copy-start.2
  160.5 3.1 %copy-start.4 = (bf16[896,1024]{1,0:T(8,128)(2,1)S(1)}, bf16[896,1024]{1,0:T(8,128)(2,1)}, u32[]{:S(2)}) copy-start(bf16[896,1024]{1,0:T(8,128)(2,1)} %get-tuple-element.17) | copy-start | bytes 5505028
  163.6 2.3 %copy-start.3 = (bf16[896,1024]{1,0:T(8,128)(2,1)S(1)}, bf16[896,1024]{1,0:T(8,128)(2,1)}, u32[]{:S(2)}) copy-start(bf16[896,1024]{1,0:T(8,128)(2,1)} %get-tuple-element.18) | copy-start | bytes 5505028
  165.9 2.3 %copy-start.6 = (bf16[512,1024]{1,0:T(8,128)(2,1)S(1)}, bf16[512,1024]{1,0:T(8,128)(2,1)}, u32[]{:S(2)}) copy-start(bf16[512,1024]{1,0:T(8,128)(2,1)} %get-tuple-element.36) | copy-start | bytes 3145732
  168.1 1.6 copy-start.5

commit v5 on v4

--- a/solution.py
+++ b/solution.py
@@ -194,7 +194,8 @@
 
 
 class Return:
-    def __init__(self, links, mail, use_grad, user, returned, crossed, ring, mine, leaving, leave_sems, land_sems):
+    def __init__(self, tag, links, mail, use_grad, user, returned, crossed, ring, mine, leaving, leave_sems, land_sems):
+        self.tag = tag
         self.links, self.mail, self.use_grad, self.user, self.returned = links, mail, use_grad, user, returned
         self.crossed, self.ring, self.mine, self.leaving = crossed, ring, mine, leaving
         self.leave_sems, self.land_sems = leave_sems, land_sems
@@ -202,14 +203,14 @@
         up, down, across = links.ids[("x", 1)], links.ids[("x", -1)], links.ids[("core", 1)]
         for side in (0, 1):
             for far_off in (2, 1, 3, 0):
-                mail.plan(("c", far_off, side), self.partner(far_off, side), self.spot(far_off, side), across)
+                mail.plan((tag, "c", far_off, side), self.partner(far_off, side), self.spot(far_off, side), across)
         slot = lambda n: (lambda: ring.at[n])
-        mail.plan("xra", self.spot(2, 0), slot(0), up)
-        mail.plan("xda", self.spot(3, 0), slot(2), down)
-        mail.plan("xrb", self.spot(2, 1), slot(1), down)
-        mail.plan("xdb", self.spot(1, 1), slot(3), up)
-        mail.plan("xsa", slot(0), slot(4), up)
-        mail.plan("xsb", slot(1), slot(5), down)
+        mail.plan((tag, "xra"), self.spot(2, 0), slot(0), up)
+        mail.plan((tag, "xda"), self.spot(3, 0), slot(2), down)
+        mail.plan((tag, "xrb"), self.spot(2, 1), slot(1), down)
+        mail.plan((tag, "xdb"), self.spot(1, 1), slot(3), up)
+        mail.plan((tag, "xsa"), slot(0), slot(4), up)
+        mail.plan((tag, "xsb"), slot(1), slot(5), down)
 
     def uses(self, side):
         return pl.ds(side * self.half, self.half)
@@ -220,37 +221,45 @@
     def partner(self, far_off, side):
         return lambda: self.use_grad.at[(self.links.x + far_off) % 4 * 2 + 1 - self.links.core, self.uses(side)]
 
-    def cross(self, side):
-        self.mail.start(*[("c", far_off, side) for far_off in (2, 1, 3, 0)])
-
-    def ring_out(self, side):
+    def cross(self):
+        self.mail.start(*[(self.tag, "c", far_off, side) for far_off in (2, 1, 3, 0) for side in (0, 1)])
+
+    def ring_out(self):
         links, mail, half = self.links, self.mail, self.half
-        first, second = (("xra", 2), ("xda", 3)) if side == 0 else (("xrb", 2), ("xdb", 1))
-        for name, far_off in (first, second, (None, 1 if side == 0 else 3), (None, 0)):
+        for far_off, names in ((2, ("xra", "xrb")), (1, (None, "xdb")), (3, ("xda", None)), (0, (None, None))):
             x = (links.x + far_off) % 4
-            mail.arrive(("c", far_off, side))
-
-            @pl.loop(side * half, (side + 1) * half)
-            def _(n):
-                self.crossed[x, n] = add(self.crossed[x, n], self.use_grad[x * 2 + links.core, n])
-
-            if name:
-                mail.start(name)
-
-    def ring_on(self, side):
+            for side, name in enumerate(names):
+                mail.arrive((self.tag, "c", far_off, side))
+
+                @pl.loop(side * half, (side + 1) * half)
+                def _(n):
+                    self.crossed[x, n] = add(self.crossed[x, n], self.use_grad[x * 2 + links.core, n])
+
+                if name:
+                    mail.start((self.tag, name))
+
+    def ring_on(self):
+        for side in (0, 1):
+            self.pass_on(side)
+
+    def ring_end(self):
+        for side in (0, 1):
+            self.finish(side)
+
+    def pass_on(self, side):
         letter, far_off = ("a", 1) if side == 0 else ("b", 3)
-        self.mail.arrive("xr" + letter)
+        self.mail.arrive((self.tag, "xr" + letter))
         own = self.spot(far_off, side)()
 
         @pl.loop(0, self.half)
         def _(n):
             self.ring[side, n] = add(self.ring[side, n], own[n])
 
-        self.mail.start("xs" + letter)
-
-    def ring_end(self, side):
+        self.mail.start((self.tag, "xs" + letter))
+
+    def finish(self, side):
         letter = "ab"[side]
-        self.mail.arrive("xd" + letter, "xs" + letter)
+        self.mail.arrive((self.tag, "xd" + letter), (self.tag, "xs" + letter))
         own = self.spot(0, side)()
 
         @pl.loop(0, self.half)
@@ -344,23 +353,29 @@
             part_key[at, columns] = total[:, :HD]
             part_value[at, columns] = total[:, HD:]
 
-    @pl.when(step >= heads)
-    def _():
-        c = step - heads
-        own = pl.ds(pl.multiple_of(c * keys, keys), keys)
-        total = jnp.zeros((keys, width), F32)
-        for h in range(heads):
-            columns = slice(h * HD, (h + 1) * HD)
-            weights = jnp.concatenate([w_key[:, columns], w_value[:, columns]], axis=1)
-            total = total + lax.dot_general(grads_kv[h, own, :], weights, NT, preferred_element_type=F32)
-        total = total.astype(BF16)
-        pieces, uses, rows = use_grad.shape[0], use_grad.shape[1] // spans, use_grad.shape[2]
-        for n in range(uses):
-            for r in range(pieces):
-                first = (n * pieces + r) * rows
-                use_grad[r, c * uses + n, :, :] = total[first:first + rows, :]
-
-
+    for part in range(len(CUTS) - 1):
+        first, last = CUTS[part], CUTS[part + 1]
+
+        @pl.when((step >= heads + part * QUARTERS) & (step < heads + (part + 1) * QUARTERS))
+        def _():
+            pieces, uses, rows = use_grad[part].shape[0], use_grad[part].shape[1] // QUARTERS, use_grad[part].shape[2]
+            c = step - heads - part * QUARTERS
+            size = panels.shape[0] // QUARTERS
+            own = pl.ds(pl.multiple_of(c * size, size), size)
+            total = jnp.zeros((size, last - first), F32)
+            for h in range(heads):
+                columns = slice(h * HD, (h + 1) * HD)
+                weights = jnp.concatenate([w_key[first:last, columns], w_value[first:last, columns]], axis=1)
+                total = total + lax.dot_general(grads_kv[h, own, :], weights, NT, preferred_element_type=F32)
+            total = total.astype(BF16)
+            for n in range(uses):
+                for r in range(pieces):
+                    at = (n * pieces + r) * rows
+                    use_grad[part][r, c * uses + n, :, :] = total[at:at + rows, :]
+
+
+QUARTERS = 4
+CUTS = (0, 512, 896)
 GROUPS = 4
 
 
@@ -376,7 +391,11 @@
         for m, (part, full, axes) in enumerate(((part_key, full_key, "yz"), (part_value, full_value, "zy"))):
             n = g * 2 + m
             items.append(Reduction(n, links, mail, part, full, g * columns, columns, axes, near.at[n], far.at[n], middle.at[n]))
-    back = Return(links, mail, use_grad, user, returned, crossed, ring, mine, leaving, leave_sems, land_sems)
+    parts = range(len(CUTS) - 1)
+    back = [
+        Return("lr"[c], links, mail, use_grad[c], user, returned[c], crossed[c], ring[c], mine[c], leaving[c], leave_sems.at[c], land_sems.at[c])
+        for c in parts
+    ]
 
     def advance(*moves):
         for g, number in moves:
@@ -393,7 +412,7 @@
 
     @pl.when(step == 0)
     def _():
-        greet(links, returned.shape[0])
+        greet(links, user.shape[0])
 
     block_step(step, spans, heads, panels, queries, cotangent, w_key, w_value, attended, grad_queries, part_key, part_value,
                use_grad, flipped, rows_kv, grads_kv, left, right, pair, stacked, wide)
@@ -404,35 +423,41 @@
         @pl.when(step == after)
         def _():
             if after == 1:
-                pl.semaphore_wait(pltpu.get_barrier_semaphore(), 3 + returned.shape[0] - 1)
+                pl.semaphore_wait(pltpu.get_barrier_semaphore(), 3 + user.shape[0] - 1)
             advance(*moves)
 
-    @pl.when(step == heads + spans // 2 - 1)
+    @pl.when(step == heads + QUARTERS - 1)
     def _():
-        back.cross(0)
+        back[0].cross()
         advance((3, 1), (2, 3), (1, 5), (0, 7))
 
-    @pl.when(step == heads + spans - 1)
+    @pl.when(step == heads + 2 * QUARTERS - 1)
     def _():
-        back.cross(1)
-        back.ring_out(0)
+        back[1].cross()
+        back[0].ring_out()
         advance((3, 2), (2, 4), (1, 6), (0, 8))
-        back.ring_out(1)
-        back.ring_on(0)
-        back.ring_on(1)
+        back[0].ring_on()
+        back[1].ring_out()
         advance((3, 3), (2, 5), (1, 7))
-        back.ring_end(0)
-        back.ring_end(1)
-        back.post()
-        advance((3, 4), (2, 6), (1, 8), (3, 5), (2, 7), (3, 6), (2, 8), (3, 7), (3, 8))
-        back.received()
-        last = pltpu.make_async_copy(returned, out_returned, out_sems.at[2 * GROUPS])
-        last.start()
+        back[0].ring_end()
+        back[0].post()
+        back[1].ring_on()
+        advance((3, 4), (2, 6), (1, 8))
+        back[1].ring_end()
+        back[1].post()
+        advance((3, 5), (2, 7), (3, 6), (2, 8), (3, 7), (3, 8))
+        last = []
+        for c in parts:
+            back[c].received()
+            target = out_returned.at[:, :, :, pl.ds(CUTS[c], CUTS[c + 1] - CUTS[c])]
+            last.append(pltpu.make_async_copy(returned[c], target, out_sems.at[2 * GROUPS + c]))
+            last[c].start()
         mail.settle()
         for g in range(GROUPS):
             result(g, 0).wait()
             result(g, 1).wait()
-        last.wait()
+        for copy in last:
+            copy.wait()
 
 
 def block_call(user, panels, queries, cotangent, w_key, w_value, racks, peers):
@@ -443,13 +468,14 @@
     rows = panel_len // racks
     total = uses * panel_len
     columns = features // GROUPS
-    messages = 2 * GROUPS * 20 + 14
+    messages = 2 * GROUPS * 20 + 28
+    cut = lambda *shape: [pltpu.VMEM(shape + (CUTS[c + 1] - CUTS[c],), BF16) for c in range(len(CUTS) - 1)]
     by_head = lambda size: pl.BlockSpec((size, HD), lambda i: (0, jnp.minimum(i, heads - 1)))
     whole = lambda a, b: pl.BlockSpec((a, b), lambda i: (0, 0), pipeline_mode=pl.Buffered(1))
     anywhere = pl.BlockSpec(memory_space=pl.ANY)
     return pl.pallas_call(
         functools.partial(block_kernel, spans, heads),
-        grid=(heads + spans,),
+        grid=(heads + 2 * QUARTERS,),
         out_shape=(
             jax.ShapeDtypeStruct(queries.shape, BF16),
             jax.ShapeDtypeStruct(queries.shape, BF16),
@@ -465,7 +491,7 @@
         scratch_shapes=[
             pltpu.VMEM((width, features), BF16),
             pltpu.VMEM((width, features), BF16),
-            pltpu.VMEM((peers, CAP, rows, width), BF16),
+            cut(peers, CAP, rows),
             pltpu.VMEM((width, total), BF16),
             pltpu.VMEM((total, 2 * HD), BF16),
             pltpu.VMEM((heads, total, 2 * HD), BF16),
@@ -476,19 +502,19 @@
             pltpu.VMEM((width, 2 * HD), BF16),
             pltpu.VMEM((width, features), BF16),
             pltpu.VMEM((width, features), BF16),
-            pltpu.VMEM((racks, uses, rows, width), BF16),
+            cut(racks, uses, rows),
             pltpu.VMEM((2 * GROUPS, 6, width // 8, columns), BF16),
             pltpu.VMEM((2 * GROUPS, 6, 64, 128), BF16),
             pltpu.VMEM((2 * GROUPS, width // 4, columns), BF16),
-            pltpu.VMEM((4, uses, rows, width), BF16),
-            pltpu.VMEM((6, uses // 2, rows, width), BF16),
-            pltpu.VMEM((uses + 1, rows, width), BF16),
-            pltpu.VMEM((peers, CAP, rows, width), BF16),
+            cut(4, uses, rows),
+            cut(6, uses // 2, rows),
+            cut(uses + 1, rows),
+            cut(peers, CAP, rows),
             pltpu.SemaphoreType.DMA((messages,)),
             pltpu.SemaphoreType.DMA((messages,)),
-            pltpu.SemaphoreType.DMA((peers,)),
-            pltpu.SemaphoreType.DMA((peers,)),
-            pltpu.SemaphoreType.DMA((2 * GROUPS + 1,)),
+            pltpu.SemaphoreType.DMA((len(CUTS) - 1, peers)),
+            pltpu.SemaphoreType.DMA((len(CUTS) - 1, peers)),
+            pltpu.SemaphoreType.DMA((2 * GROUPS + 2,)),
         ],
         compiler_params=pltpu.CompilerParams(
             collective_id=1, has_side_effects=True, vmem_limit_bytes=58 * 1024 * 1024
@@ -615,9 +641,6 @@
     mail.settle()
 
 
-CUTS = (0, 512, 896)
-
-
 def fetch_call(owners, slots, database, peers, racks):
     uses = owners.shape[0] * owners.shape[1]
     local_rows, panel_len, width = database.shape
@@ -635,7 +658,7 @@
             jax.ShapeDtypeStruct((peers, 1, 128), jnp.int32),
             jax.ShapeDtypeStruct((peers, 1, 128), jnp.int32),
         ),
-        in_specs=[smem, smem, anywhere],
+        in_specs=[smem, smem, pl.BlockSpec(memory_space=pltpu.HBM)],
         out_specs=(anywhere, vmem, vmem),
         scratch_shapes=[
             pltpu.VMEM((local_rows, rows, width), BF16),

time: 171 us -> 163 us (0.953)
  Pallas kernels: 153 us -> 144 us
    pallas_call x1, Pallas kernels: 107 us -> 99.1 us  [block_call(): pl.pallas_call(functools.partial(block_kernel, spans, heads), grid=(heads...]
where the time goes in v5:
time: 163 us; the launch traced here: 162 us
  Pallas kernels  144 us (88%)
  local copies, waits for them, and re-layouts  10.9 us (7%)
  other arithmetic  4.5 us (3%)
  matrix products  1.86 us (1%)
    pallas_call x1, Pallas kernels, block_call(): pl.pallas_call(functools.partial(block_kernel, spans, heads), grid=(heads...  99.1 us
    pallas_call x1, Pallas kernels, fetch_call(): pl.pallas_call(functools.partial(fetch_kernel, CUTS), out_shape=(jax.Shap...  45.4 us
    unnamed x19, local copies, waits for them, and re-layouts  10.8 us
    convert_element_type x2, other arithmetic, local(): grad_w_key, grad_w_value = (full_key.astype(F32), full_value.astype(F32))  4.5 us

profile of v5, /device:TPU:0, one launch (start us, length us, event | category | flops | bytes accessed | tf_op | source)
XLA Modules:
  0.0 162.5 jit_solution(3958610806809800077)
XLA Ops:
  0.6 0.8 copy.16.owners
  1.4 0.8 copy.17.slots
  2.1 0.0 copy-start
  2.1 3.1 %copy-done = bf16[32,128,896]{2,1,0:T(8,128)(2,1)S(1)} copy-done((bf16[32,128,896]{2,1,0:T(8,128)(2,1)S(1)}, bf16[32,128,896]{2,1,0:T(8,128)(2,1)}, u32[]{:S(2)}) %copy-start) | copy-done | bytes 7340056
  5.2 45.4 %fetch.1 = (bf16[16,128,896]{2,1,0:T(8,128)(2,1)S(1)}, s32[16,1,128]{2,1,0:T(1,128)S(1)}, s32[16,1,128]{2,1,0:T(1,128)S(1)}) custom-call(s32[8,2]{1,0:T(8,128)S(1)} %copy.16.owners, s32[8,2]{1,0:T(8,128)S(1)} %copy.17.slots, bf16[32,128,896]{2,1,0:T(8,128)(2,1)S(1)} %copy-done), custom_call_target="tpu_custom_call" | custom-call | tf_op jit(solution)/shard_map/fetch/pallas_call | solution.py:654
  50.6 0.0 copy-start.1
  50.6 1.8 %copy-done.1 = bf16[16,128,896]{2,1,0:T(8,128)(2,1)} copy-done((bf16[16,128,896]{2,1,0:T(8,128)(2,1)}, bf16[16,128,896]{2,1,0:T(8,128)(2,1)S(1)}, u32[]{:S(2)}) %copy-start.1) | copy-done | bytes 3670040
  52.5 0.0 copy-start.2
  52.5 0.6 copy-done.2
  53.1 0.1 eq.15
  53.2 99.1 %block.1 = (bf16[512,1024]{1,0:T(8,128)(2,1)}, bf16[512,1024]{1,0:T(8,128)(2,1)}, bf16[896,1024]{1,0:T(8,128)(2,1)}, bf16[896,1024]{1,0:T(8,128)(2,1)}, bf16[16,3,16,896]{3,2,1,0:T(8,128)(2,1)}) custom-call(s32[16,1,128]{2,1,0:T(1,128)} %copy-done.2, bf16[2048,896]{1,0:T(8,128)(2,1)} %bitcast.5, bf16[512,1024]{1,0:T(8,128)(2,1)} %queries.1, ...), custom_call_target="tpu_custom_call" | custom-call | tf_op jit(solution)/shard_map/block/pallas_call | solution.py:476
  152.3 0.0 copy-start.4
  152.3 1.9 %convolution_convert_fusion = bf16[32,16,896]{2,0,1:T(8,128)(2,1)S(1)} fusion(bf16[48,16,896]{2,1,0:T(8,128)(2,1)} %bitcast.6, s32[48]{0:T(128)S(1)} %eq.15), kind=kOutput, calls=%fused_computation | convolution fusion | flops 44500480 | bytes 2293952 | tf_op jit(solution)/shard_map/ns,spw->npw/dot_general | solution.py:681
  154.2 1.2 copy.19
  155.4 0.0 copy-done.4
  155.4 0.0 copy-start.3
  155.4 2.3 %convert_element_type.10 = f32[896,1024]{1,0:T(8,128)} convert(bf16[896,1024]{1,0:T(8,128)(2,1)S(1)} %copy-done.4) | non-fusion elementwise | flops 917504 | bytes 5505024 | tf_op jit(solution)/shard_map/convert_element_type | solution.py:695
  157.6 0.0 copy-done.3
  157.6 0.0 copy-start.6
  157.6 2.3 %convert_element_type.11 = f32[896,1024]{1,0:T(8,128)} convert(bf16[896,1024]{1,0:T(8,128)(2,1)S(1)} %copy-done.3) | non-fusion elementwise | flops 917504 | bytes 5505024 | tf_op jit(solution)/shard_map/convert_element_type | solution.py:695
  159.9 0.0 copy-done.6
  159.9 1.0 copy.24
  160.9 0.6 copy-done.5
  161.5 1.0 copy.25
  (2 shorter events, 0.0 us)
Async XLA Ops:
  2.1 3.1 %copy-start = (bf16[32,128,896]{2,1,0:T(8,128)(2,1)S(1)}, bf16[32,128,896]{2,1,0:T(8,128)(2,1)}, u32[]{:S(2)}) copy-start(bf16[32,128,896]{2,1,0:T(8,128)(2,1)} %database.1) | copy-start | bytes 22020100
  50.6 1.8 %copy-start.1 = (bf16[16,128,896]{2,1,0:T(8,128)(2,1)}, bf16[16,128,896]{2,1,0:T(8,128)(2,1)S(1)}, u32[]{:S(2)}) copy-start(bf16[16,128,896]{2,1,0:T(8,128)(2,1)S(1)} %get-tuple-element.14) | copy-start | bytes 11010052
  52.5 0.6 copy-start.2
  152.3 3.1 %copy-start.4 = (bf16[896,1024]{1,0:T(8,128)(2,1)S(1)}, bf16[896,1024]{1,0:T(8,128)(2,1)}, u32[]{:S(2)}) copy-start(bf16[896,1024]{1,0:T(8,128)(2,1)} %get-tuple-element.17) | copy-start | bytes 5505028
  155.4 2.3 %copy-start.3 = (bf16[896,1024]{1,0:T(8,128)(2,1)S(1)}, bf16[896,1024]{1,0:T(8,128)(2,1)}, u32[]{:S(2)}) copy-start(bf16[896,1024]{1,0:T(8,128)(2,1)} %get-tuple-element.18) | copy-start | bytes 5505028
  157.6 2.3 %copy-start.6 = (bf16[512,1024]{1,0:T(8,128)(2,1)S(1)}, bf16[512,1024]{1,0:T(8,128)(2,1)}, u32[]{:S(2)}) copy-start(bf16[512,1024]{1,0:T(8,128)(2,1)} %get-tuple-element.36) | copy-start | bytes 3145732
  159.9 1.6 copy-start.5

commit v6 on v5

--- a/solution.py
+++ b/solution.py
@@ -11,7 +11,7 @@
 SPAN = 64
 CAP = 3
 PARTS = 2
-GPARTS = 2
+GPARTS = 1
 NT = (((1,), (1,)), ((), ()))
 TN = (((0,), (0,)), ((), ()))
 F32 = jnp.float32
@@ -348,10 +348,12 @@
         @pl.loop(0, GPARTS)
         def _(n):
             size = width // GPARTS
+            share = part_key.shape[2] // HD
+            pair_of, column_of = step // share, pl.ds(pl.multiple_of(step % share * HD, HD), HD)
             at = pl.ds(pl.multiple_of(n * size, size), size)
             total = dot(flipped[at, :], grads_kv[step]).astype(BF16)
-            part_key[at, columns] = total[:, :HD]
-            part_value[at, columns] = total[:, HD:]
+            part_key[pair_of, at, column_of] = total[:, :HD]
+            part_value[pair_of, at, column_of] = total[:, HD:]
 
     for part in range(len(CUTS) - 1):
         first, last = CUTS[part], CUTS[part + 1]
@@ -385,12 +387,12 @@
     step = pl.program_id(0)
     links = Links(4, 4, 4)
     mail = Mail(send_sems, recv_sems)
-    columns = part_key.shape[1] // GROUPS
+    columns = part_key.shape[2]
     items = []
     for g in range(GROUPS):
         for m, (part, full, axes) in enumerate(((part_key, full_key, "yz"), (part_value, full_value, "zy"))):
             n = g * 2 + m
-            items.append(Reduction(n, links, mail, part, full, g * columns, columns, axes, near.at[n], far.at[n], middle.at[n]))
+            items.append(Reduction(n, links, mail, part.at[g], full.at[g], 0, columns, axes, near.at[n], far.at[n], middle.at[n]))
     parts = range(len(CUTS) - 1)
     back = [
         Return("lr"[c], links, mail, use_grad[c], user, returned[c], crossed[c], ring[c], mine[c], leaving[c], leave_sems.at[c], land_sems.at[c])
@@ -407,8 +409,7 @@
 
     def result(g, m):
         source, target = ((full_key, out_key), (full_value, out_value))[m]
-        at = (slice(None), pl.ds(g * columns, columns))
-        return pltpu.make_async_copy(source.at[at], target.at[at], out_sems.at[2 * g + m])
+        return pltpu.make_async_copy(source.at[g], target.at[:, pl.ds(g * columns, columns)], out_sems.at[2 * g + m])
 
     @pl.when(step == 0)
     def _():
@@ -426,7 +427,7 @@
                 pl.semaphore_wait(pltpu.get_barrier_semaphore(), 3 + user.shape[0] - 1)
             advance(*moves)
 
-    @pl.when(step == heads + QUARTERS - 1)
+    @pl.when(step == heads + 3)
     def _():
         back[0].cross()
         advance((3, 1), (2, 3), (1, 5), (0, 7))
@@ -436,16 +437,19 @@
         back[1].cross()
         back[0].ring_out()
         advance((3, 2), (2, 4), (1, 6), (0, 8))
+        advance((3, 3), (2, 5), (1, 7))
         back[0].ring_on()
         back[1].ring_out()
-        advance((3, 3), (2, 5), (1, 7))
+        advance((3, 4), (2, 6), (1, 8))
+        advance((3, 5), (2, 7))
         back[0].ring_end()
+        advance((3, 6), (2, 8))
         back[0].post()
         back[1].ring_on()
-        advance((3, 4), (2, 6), (1, 8))
+        advance((3, 7))
         back[1].ring_end()
         back[1].post()
-        advance((3, 5), (2, 7), (3, 6), (2, 8), (3, 7), (3, 8))
+        advance((3, 8))
         last = []
         for c in parts:
             back[c].received()
@@ -489,8 +493,8 @@
         ],
         out_specs=[by_head(queries.shape[0]), by_head(queries.shape[0]), anywhere, anywhere, anywhere],
         scratch_shapes=[
-            pltpu.VMEM((width, features), BF16),
-            pltpu.VMEM((width, features), BF16),
+            pltpu.VMEM((GROUPS, width, columns), BF16),
+            pltpu.VMEM((GROUPS, width, columns), BF16),
             cut(peers, CAP, rows),
             pltpu.VMEM((width, total), BF16),
             pltpu.VMEM((total, 2 * HD), BF16),
@@ -500,8 +504,8 @@
             pltpu.VMEM((spans, 2 * SPAN, total // spans), F32),
             pltpu.VMEM((spans, 2 * SPAN, total // spans), BF16),
             pltpu.VMEM((width, 2 * HD), BF16),
-            pltpu.VMEM((width, features), BF16),
-            pltpu.VMEM((width, features), BF16),
+            pltpu.VMEM((GROUPS, width, columns), BF16),
+            pltpu.VMEM((GROUPS, width, columns), BF16),
             cut(racks, uses, rows),
             pltpu.VMEM((2 * GROUPS, 6, width // 8, columns), BF16),
             pltpu.VMEM((2 * GROUPS, 6, 64, 128), BF16),
@@ -671,7 +675,7 @@
             sems((9 * parts,)), sems((9 * parts,)),
         ],
         compiler_params=pltpu.CompilerParams(
-            collective_id=0, has_side_effects=True, vmem_limit_bytes=24 * 1024 * 1024
+            collective_id=0, has_side_effects=True, vmem_limit_bytes=58 * 1024 * 1024
         ),
         name="fetch",
     )(owners, slots, database)

time: 163 us -> 154 us (0.945)
  Pallas kernels: 144 us -> 139 us
  local copies, waits for them, and re-layouts: 10.9 us -> 7.28 us
    pallas_call x1, Pallas kernels: 99.1 us -> 92.2 us  [block_call(): pl.pallas_call(functools.partial(block_kernel, spans, heads), grid=(heads...]
    unnamed x19 -> x13, local copies, waits for them, and re-layouts: 10.8 us -> 6.48 us
where the time goes in v6:
time: 154 us; the launch traced here: 153 us
  Pallas kernels  139 us (90%)
  local copies, waits for them, and re-layouts  7.28 us (5%)
  other arithmetic  4.5 us (3%)
  matrix products  1.86 us (1%)
    pallas_call x1, Pallas kernels, block_call(): pl.pallas_call(functools.partial(block_kernel, spans, heads), grid=(heads...  92.2 us
    pallas_call x1, Pallas kernels, fetch_call(): pl.pallas_call(functools.partial(fetch_kernel, CUTS), out_shape=(jax.Shap...  46.8 us
    unnamed x13, local copies, waits for them, and re-layouts  6.48 us
    convert_element_type x2, other arithmetic, local(): grad_w_key, grad_w_value = (full_key.astype(F32), full_value.astype(F32))  4.5 us

profile of v6, /device:TPU:0, one launch (start us, length us, event | category | flops | bytes accessed | tf_op | source)
XLA Modules:
  0.0 153.4 jit_solution(1842490913132040055)
XLA Ops:
  0.6 1.3 copy.16.owners
  2.0 1.3 copy.17.slots
  3.3 46.8 %fetch.1 = (bf16[16,128,896]{2,1,0:T(8,128)(2,1)}, s32[16,1,128]{2,1,0:T(1,128)}, s32[16,1,128]{2,1,0:T(1,128)}) custom-call(s32[8,2]{1,0:T(8,128)} %copy.16.owners, s32[8,2]{1,0:T(8,128)} %copy.17.slots, bf16[32,128,896]{2,1,0:T(8,128)(2,1)} %database.1), custom_call_target="tpu_custom_call" | custom-call | tf_op jit(solution)/shard_map/fetch/pallas_call | solution.py:658
  50.2 0.7 slice_reduce_fusion
  50.9 0.1 eq.15
  51.0 92.2 %block.1 = (bf16[512,1024]{1,0:T(8,128)(2,1)}, bf16[512,1024]{1,0:T(8,128)(2,1)}, bf16[896,1024]{1,0:T(8,128)(2,1)}, bf16[896,1024]{1,0:T(8,128)(2,1)}, bf16[16,3,16,896]{3,2,1,0:T(8,128)(2,1)}) custom-call(s32[16,1,128]{2,1,0:T(1,128)} %get-tuple-element.13.user, bf16[2048,896]{1,0:T(8,128)(2,1)} %bitcast.5, bf16[512,1024]{1,0:T(8,128)(2,1)} %queries.1, ...), custom_call_target="tpu_custom_call" | custom-call | tf_op jit(solution)/shard_map/block/pallas_call | solution.py:480
  143.2 0.0 copy-start.1
  143.2 1.9 %convolution_convert_fusion = bf16[32,16,896]{2,0,1:T(8,128)(2,1)S(1)} fusion(bf16[48,16,896]{2,1,0:T(8,128)(2,1)} %bitcast.6, s32[48]{0:T(128)S(1)} %eq.15), kind=kOutput, calls=%fused_computation | convolution fusion | flops 44500480 | bytes 2293952 | tf_op jit(solution)/shard_map/ns,spw->npw/dot_general | solution.py:685
  145.1 1.2 copy.19
  146.3 0.0 copy-done.1
  146.3 0.0 copy-start
  146.3 2.3 %convert_element_type.10 = f32[896,1024]{1,0:T(8,128)} convert(bf16[896,1024]{1,0:T(8,128)(2,1)S(1)} %copy-done.1) | non-fusion elementwise | flops 917504 | bytes 5505024 | tf_op jit(solution)/shard_map/convert_element_type | solution.py:699
  148.5 0.0 copy-done
  148.5 0.0 copy-start.3
  148.5 2.3 %convert_element_type.11 = f32[896,1024]{1,0:T(8,128)} convert(bf16[896,1024]{1,0:T(8,128)(2,1)S(1)} %copy-done) | non-fusion elementwise | flops 917504 | bytes 5505024 | tf_op jit(solution)/shard_map/convert_element_type | solution.py:699
  150.8 0.0 copy-done.3
  150.8 0.0 copy-start.2
  150.8 1.0 copy.24
  151.8 0.6 copy-done.2
  152.4 1.0 copy.25
Async XLA Ops:
  143.2 3.1 %copy-start.1 = (bf16[896,1024]{1,0:T(8,128)(2,1)S(1)}, bf16[896,1024]{1,0:T(8,128)(2,1)}, u32[]{:S(2)}) copy-start(bf16[896,1024]{1,0:T(8,128)(2,1)} %get-tuple-element.17) | copy-start | bytes 5505028
  146.3 2.3 %copy-start = (bf16[896,1024]{1,0:T(8,128)(2,1)S(1)}, bf16[896,1024]{1,0:T(8,128)(2,1)}, u32[]{:S(2)}) copy-start(bf16[896,1024]{1,0:T(8,128)(2,1)} %get-tuple-element.18) | copy-start | bytes 5505028
  148.5 2.3 %copy-start.3 = (bf16[512,1024]{1,0:T(8,128)(2,1)S(1)}, bf16[512,1024]{1,0:T(8,128)(2,1)}, u32[]{:S(2)}) copy-start(bf16[512,1024]{1,0:T(8,128)(2,1)} %get-tuple-element.36) | copy-start | bytes 3145732
  150.8 1.6 %copy-start.2 = (bf16[512,1024]{1,0:T(8,128)(2,1)S(1)}, bf16[512,1024]{1,0:T(8,128)(2,1)}, u32[]{:S(2)}) copy-start(bf16[512,1024]{1,0:T(8,128)(2,1)} %get-tuple-element.37) | copy-start | bytes 3145732

commit v7 on v6

--- a/solution.py
+++ b/solution.py
@@ -293,7 +293,7 @@
         )
 
 
-def block_step(step, spans, heads, panels, queries, cotangent, w_key, w_value, attended, grad_queries, part_key, part_value,
+def block_step(step, spans, heads, panels, queries, cotangent, head_key, head_value, w_key, w_value, attended, grad_queries, part_key, part_value,
                use_grad, flipped, rows_kv, grads_kv, left, right, pair, stacked, wide):
     keys = panels.shape[0] // spans
     width = panels.shape[1]
@@ -308,9 +308,8 @@
 
     @pl.when(step < heads)
     def _():
-        columns = pl.ds(pl.multiple_of(step * HD, HD), HD)
-        wide[:, :HD] = w_key[:, columns]
-        wide[:, HD:] = w_value[:, columns]
+        wide[:, :HD] = head_key[...]
+        wide[:, HD:] = head_value[...]
 
         @pl.loop(0, PARTS)
         def _(n):
@@ -381,10 +380,13 @@
 GROUPS = 4
 
 
-def block_kernel(spans, heads, user, panels, queries, cotangent, w_key, w_value, attended, grad_queries, out_key, out_value,
-                 out_returned, full_key, full_value, returned, flipped, rows_kv, grads_kv, left, right, pair, stacked, wide, part_key, part_value, use_grad, near, far,
-                 middle, crossed, ring, mine, leaving, send_sems, recv_sems, leave_sems, land_sems, out_sems):
+def block_kernel(spans, heads, user, panels, queries, cotangent, head_key, head_value, all_key, all_value, attended, grad_queries,
+                 out_key, out_value, out_returned, w_key, w_value, full_key, full_value, returned, flipped, rows_kv, grads_kv, left, right, pair, stacked, wide, part_key, part_value, use_grad, near, far,
+                 middle, crossed, ring, mine, leaving, send_sems, recv_sems, leave_sems, land_sems, out_sems, weight_sems):
     step = pl.program_id(0)
+    weights = [
+        pltpu.make_async_copy(all_key, w_key, weight_sems.at[0]), pltpu.make_async_copy(all_value, w_value, weight_sems.at[1])
+    ]
     links = Links(4, 4, 4)
     mail = Mail(send_sems, recv_sems)
     columns = part_key.shape[2]
@@ -415,7 +417,17 @@
     def _():
         greet(links, user.shape[0])
 
-    block_step(step, spans, heads, panels, queries, cotangent, w_key, w_value, attended, grad_queries, part_key, part_value,
+    @pl.when(step == 0)
+    def _():
+        for copy in weights:
+            copy.start()
+
+    @pl.when(step == heads)
+    def _():
+        for copy in weights:
+            copy.wait()
+
+    block_step(step, spans, heads, panels, queries, cotangent, head_key, head_value, w_key, w_value, attended, grad_queries, part_key, part_value,
                use_grad, flipped, rows_kv, grads_kv, left, right, pair, stacked, wide)
 
     for after in range(1, heads):
@@ -489,10 +501,12 @@
         ),
         in_specs=[
             pl.BlockSpec(memory_space=pltpu.SMEM), whole(total, width), by_head(queries.shape[0]), by_head(queries.shape[0]),
-            whole(width, features), whole(width, features),
+            by_head(width), by_head(width), anywhere, anywhere,
         ],
         out_specs=[by_head(queries.shape[0]), by_head(queries.shape[0]), anywhere, anywhere, anywhere],
         scratch_shapes=[
+            pltpu.VMEM((width, features), BF16),
+            pltpu.VMEM((width, features), BF16),
             pltpu.VMEM((GROUPS, width, columns), BF16),
             pltpu.VMEM((GROUPS, width, columns), BF16),
             cut(peers, CAP, rows),
@@ -519,21 +533,22 @@
             pltpu.SemaphoreType.DMA((len(CUTS) - 1, peers)),
             pltpu.SemaphoreType.DMA((len(CUTS) - 1, peers)),
             pltpu.SemaphoreType.DMA((2 * GROUPS + 2,)),
+            pltpu.SemaphoreType.DMA((2,)),
         ],
         compiler_params=pltpu.CompilerParams(
             collective_id=1, has_side_effects=True, vmem_limit_bytes=58 * 1024 * 1024
         ),
         name="block",
-    )(user, panels.reshape(total, width), queries, cotangent, w_key, w_value)
-
-
-def fetch_kernel(cuts, owners, slots, database, panels, asked, user, stored, wanted, heard, leaving, landing, mine, load_sem, ask_send,
+    )(user, panels.reshape(total, width), queries, cotangent, w_key, w_value, w_key, w_value)
+
+
+def fetch_kernel(cuts, named_rows, database, panels, asked, user, stored, wanted, heard, leaving, landing, mine, load_sem, ask_send,
                  ask_recv, leave_sems, land_sems, own_sems, send_sems, recv_sems):
     links = Links(4, 4, 4)
     peers = asked.shape[0]
     local_rows, _, width = stored.shape
     uses, rows = mine.shape[0], mine.shape[1]
-    nbrs = owners.shape[1]
+    nbrs = named_rows.shape[1] // 2
     my_rows = lambda x, core: pl.ds(pl.multiple_of((x * 2 + core) * rows, rows), rows)
     load = pltpu.make_async_copy(database.at[:, my_rows(links.x, links.core), :], stored, load_sem.at[0])
     load.start()
@@ -546,9 +561,9 @@
     rows_wanted = jnp.full((peers, 1, 128), local_rows, jnp.int32)
     users = jnp.full((peers, 1, 128), uses, jnp.int32)
     for u in range(uses):
-        named = peer_of == owners[u // nbrs, u % nbrs]
+        named = peer_of == named_rows[u // nbrs, u % nbrs]
         here = named & (lane == seen)
-        rows_wanted = jnp.where(here, slots[u // nbrs, u % nbrs], rows_wanted)
+        rows_wanted = jnp.where(here, named_rows[u // nbrs, nbrs + u % nbrs], rows_wanted)
         users = jnp.where(here, u, users)
         seen = seen + named.astype(jnp.int32)
     wanted[...] = rows_wanted
@@ -620,10 +635,10 @@
     for c in range(count):
         pl.loop(1, peers)(lambda far: answer(c, far).wait())
         for u in range(uses):
-            owner = owners[u // nbrs, u % nbrs]
+            owner = named_rows[u // nbrs, u % nbrs]
             rank = jnp.int32(0)
             for v in range(u):
-                rank = rank + (owners[v // nbrs, v % nbrs] == owner).astype(jnp.int32)
+                rank = rank + (named_rows[v // nbrs, v % nbrs] == owner).astype(jnp.int32)
             mine[u, :, cuts[c]:cuts[c + 1]] = landing[c][owner, jnp.minimum(rank, CAP - 1)]
         source = mine.at[:, :, pl.ds(cuts[c], cuts[c + 1] - cuts[c])]
         target = out(c, 0, 0, uses)
@@ -662,7 +677,7 @@
             jax.ShapeDtypeStruct((peers, 1, 128), jnp.int32),
             jax.ShapeDtypeStruct((peers, 1, 128), jnp.int32),
         ),
-        in_specs=[smem, smem, pl.BlockSpec(memory_space=pltpu.HBM)],
+        in_specs=[smem, pl.BlockSpec(memory_space=pltpu.HBM)],
         out_specs=(anywhere, vmem, vmem),
         scratch_shapes=[
             pltpu.VMEM((local_rows, rows, width), BF16),
@@ -678,7 +693,7 @@
             collective_id=0, has_side_effects=True, vmem_limit_bytes=58 * 1024 * 1024
         ),
         name="fetch",
-    )(owners, slots, database)
+    )(jnp.concatenate([owners, slots], axis=1), database)
 
 
 def pick(selector, source):

time: 154 us -> 152 us (0.987)
  no operation moved by 1% of the time
where the time goes in v7:
time: 152 us
  Pallas kernels  138 us (91%)
  local copies, waits for them, and re-layouts  6.1 us (4%)
  other arithmetic  5.17 us (3%)
  matrix products  1.86 us (1%)
    pallas_call x1, Pallas kernels, block_call(): pl.pallas_call(functools.partial(block_kernel, spans, heads), grid=(heads...  91.2 us
    pallas_call x1, Pallas kernels, fetch_call(): pl.pallas_call(functools.partial(fetch_kernel, CUTS), out_shape=(jax.Shap...  46.8 us
    unnamed x13, local copies, waits for them, and re-layouts  5.29 us
    convert_element_type x2, other arithmetic, local(): grad_w_key, grad_w_value = (full_key.astype(F32), full_value.astype(F32))  4.5 us

profile of v7, /device:TPU:0, one launch (start us, length us, event | category | flops | bytes accessed | tf_op | source)
XLA Modules:
  0.0 151.8 jit_solution(1841884609178836489)
XLA Ops:
  0.6 0.8 copy.16
  1.4 0.8 copy.17
  2.1 0.7 pad_add_fusion.named_rows
  2.8 46.8 %fetch.1 = (bf16[16,128,896]{2,1,0:T(8,128)(2,1)}, s32[16,1,128]{2,1,0:T(1,128)}, s32[16,1,128]{2,1,0:T(1,128)}) custom-call(s32[8,4]{1,0:T(8,128)} %pad_add_fusion.named_rows, bf16[32,128,896]{2,1,0:T(8,128)(2,1)} %database.1), custom_call_target="tpu_custom_call" | custom-call | tf_op jit(solution)/shard_map/fetch/pallas_call | solution.py:673
  49.6 0.7 slice_reduce_fusion
  50.3 0.1 eq.15
  50.4 91.2 %block.1 = (bf16[512,1024]{1,0:T(8,128)(2,1)}, bf16[512,1024]{1,0:T(8,128)(2,1)}, bf16[896,1024]{1,0:T(8,128)(2,1)}, bf16[896,1024]{1,0:T(8,128)(2,1)}, bf16[16,3,16,896]{3,2,1,0:T(8,128)(2,1)}) custom-call(s32[16,1,128]{2,1,0:T(1,128)} %get-tuple-element.13.user, bf16[2048,896]{1,0:T(8,128)(2,1)} %bitcast.5, bf16[512,1024]{1,0:T(8,128)(2,1)} %queries.1, ...), custom_call_target="tpu_custom_call" | custom-call | tf_op jit(solution)/shard_map/block/pallas_call | solution.py:492
  141.6 0.0 copy-start.1
  141.6 1.9 %convolution_convert_fusion = bf16[32,16,896]{2,0,1:T(8,128)(2,1)S(1)} fusion(bf16[48,16,896]{2,1,0:T(8,128)(2,1)} %bitcast.6, s32[48]{0:T(128)S(1)} %eq.15), kind=kOutput, calls=%fused_computation | convolution fusion | flops 44500480 | bytes 2293952 | tf_op jit(solution)/shard_map/ns,spw->npw/dot_general | solution.py:700
  143.5 1.2 copy.19
  144.7 0.0 copy-done.1
  144.7 0.0 copy-start
  144.7 2.3 %convert_element_type.10 = f32[896,1024]{1,0:T(8,128)} convert(bf16[896,1024]{1,0:T(8,128)(2,1)S(1)} %copy-done.1) | non-fusion elementwise | flops 917504 | bytes 5505024 | tf_op jit(solution)/shard_map/convert_element_type | solution.py:714
  146.9 0.0 copy-done
  146.9 0.0 copy-start.3
  146.9 2.3 %convert_element_type.11 = f32[896,1024]{1,0:T(8,128)} convert(bf16[896,1024]{1,0:T(8,128)(2,1)S(1)} %copy-done) | non-fusion elementwise | flops 917504 | bytes 5505024 | tf_op jit(solution)/shard_map/convert_element_type | solution.py:714
  149.2 0.0 copy-done.3
  149.2 0.0 copy-start.2
  149.2 1.0 copy.24
  150.2 0.6 copy-done.2
  150.8 1.0 copy.25
Async XLA Ops:
  141.6 3.1 %copy-start.1 = (bf16[896,1024]{1,0:T(8,128)(2,1)S(1)}, bf16[896,1024]{1,0:T(8,128)(2,1)}, u32[]{:S(2)}) copy-start(bf16[896,1024]{1,0:T(8,128)(2,1)} %get-tuple-element.17) | copy-start | bytes 5505028
  144.7 2.3 %copy-start = (bf16[896,1024]{1,0:T(8,128)(2,1)S(1)}, bf16[896,1024]{1,0:T(8,128)(2,1)}, u32[]{:S(2)}) copy-start(bf16[896,1024]{1,0:T(8,128)(2,1)} %get-tuple-element.18) | copy-start | bytes 5505028
  146.9 2.3 %copy-start.3 = (bf16[512,1024]{1,0:T(8,128)(2,1)S(1)}, bf16[512,1024]{1,0:T(8,128)(2,1)}, u32[]{:S(2)}) copy-start(bf16[512,1024]{1,0:T(8,128)(2,1)} %get-tuple-element.36) | copy-start | bytes 3145732
  149.2 1.6 %copy-start.2 = (bf16[512,1024]{1,0:T(8,128)(2,1)S(1)}, bf16[512,1024]{1,0:T(8,128)(2,1)}, u32[]{:S(2)}) copy-start(bf16[512,1024]{1,0:T(8,128)(2,1)} %get-tuple-element.37) | copy-start | bytes 3145732

commit v8 on v7

--- a/solution.py
+++ b/solution.py
@@ -375,7 +375,7 @@
                     use_grad[part][r, c * uses + n, :, :] = total[at:at + rows, :]
 
 
-QUARTERS = 4
+QUARTERS = 2
 CUTS = (0, 512, 896)
 GROUPS = 4
 
@@ -439,7 +439,7 @@
                 pl.semaphore_wait(pltpu.get_barrier_semaphore(), 3 + user.shape[0] - 1)
             advance(*moves)
 
-    @pl.when(step == heads + 3)
+    @pl.when(step == heads + QUARTERS - 1)
     def _():
         back[0].cross()
         advance((3, 1), (2, 3), (1, 5), (0, 7))

time: 152 us -> 151 us (level)
  no operation moved by 1% of the time
where the time goes in v8:
time: 151 us
  Pallas kernels  137 us (91%)
  local copies, waits for them, and re-layouts  6.1 us (4%)
  other arithmetic  5.17 us (3%)
  matrix products  1.87 us (1%)
    pallas_call x1, Pallas kernels, block_call(): pl.pallas_call(functools.partial(block_kernel, spans, heads), grid=(heads...  90.5 us
    pallas_call x1, Pallas kernels, fetch_call(): pl.pallas_call(functools.partial(fetch_kernel, CUTS), out_shape=(jax.Shap...  46.8 us
    unnamed x13, local copies, waits for them, and re-layouts  5.29 us
    convert_element_type x2, other arithmetic, local(): grad_w_key, grad_w_value = (full_key.astype(F32), full_value.astype(F32))  4.5 us

profile of v8, /device:TPU:0, one launch (start us, length us, event | category | flops | bytes accessed | tf_op | source)
XLA Modules:
  0.0 151.1 jit_solution(2057845683198149924)
XLA Ops:
  0.6 0.8 copy.16
  1.4 0.8 copy.17
  2.1 0.7 pad_add_fusion.named_rows
  2.8 46.8 %fetch.1 = (bf16[16,128,896]{2,1,0:T(8,128)(2,1)}, s32[16,1,128]{2,1,0:T(1,128)}, s32[16,1,128]{2,1,0:T(1,128)}) custom-call(s32[8,4]{1,0:T(8,128)} %pad_add_fusion.named_rows, bf16[32,128,896]{2,1,0:T(8,128)(2,1)} %database.1), custom_call_target="tpu_custom_call" | custom-call | tf_op jit(solution)/shard_map/fetch/pallas_call | solution.py:673
  49.6 0.7 slice_reduce_fusion
  50.3 0.1 eq.15
  50.4 90.5 %block.1 = (bf16[512,1024]{1,0:T(8,128)(2,1)}, bf16[512,1024]{1,0:T(8,128)(2,1)}, bf16[896,1024]{1,0:T(8,128)(2,1)}, bf16[896,1024]{1,0:T(8,128)(2,1)}, bf16[16,3,16,896]{3,2,1,0:T(8,128)(2,1)}) custom-call(s32[16,1,128]{2,1,0:T(1,128)} %get-tuple-element.13.user, bf16[2048,896]{1,0:T(8,128)(2,1)} %bitcast.5, bf16[512,1024]{1,0:T(8,128)(2,1)} %queries.1, ...), custom_call_target="tpu_custom_call" | custom-call | tf_op jit(solution)/shard_map/block/pallas_call | solution.py:492
  140.9 0.0 copy-start.1
  140.9 1.9 %convolution_convert_fusion = bf16[32,16,896]{2,0,1:T(8,128)(2,1)S(1)} fusion(bf16[48,16,896]{2,1,0:T(8,128)(2,1)} %bitcast.6, s32[48]{0:T(128)S(1)} %eq.15), kind=kOutput, calls=%fused_computation | convolution fusion | flops 44500480 | bytes 2293952 | tf_op jit(solution)/shard_map/ns,spw->npw/dot_general | solution.py:700
  142.8 1.2 copy.19
  144.0 0.0 copy-done.1
  144.0 0.0 copy-start
  144.0 2.3 %convert_element_type.10 = f32[896,1024]{1,0:T(8,128)} convert(bf16[896,1024]{1,0:T(8,128)(2,1)S(1)} %copy-done.1) | non-fusion elementwise | flops 917504 | bytes 5505024 | tf_op jit(solution)/shard_map/convert_element_type | solution.py:714
  146.2 0.0 copy-done
  146.2 0.0 copy-start.3
  146.2 2.3 %convert_element_type.11 = f32[896,1024]{1,0:T(8,128)} convert(bf16[896,1024]{1,0:T(8,128)(2,1)S(1)} %copy-done) | non-fusion elementwise | flops 917504 | bytes 5505024 | tf_op jit(solution)/shard_map/convert_element_type | solution.py:714
  148.5 0.0 copy-done.3
  148.5 0.0 copy-start.2
  148.5 1.0 copy.24
  149.4 0.6 copy-done.2
  150.1 1.0 copy.25
Async XLA Ops:
  140.9 3.1 %copy-start.1 = (bf16[896,1024]{1,0:T(8,128)(2,1)S(1)}, bf16[896,1024]{1,0:T(8,128)(2,1)}, u32[]{:S(2)}) copy-start(bf16[896,1024]{1,0:T(8,128)(2,1)} %get-tuple-element.17) | copy-start | bytes 5505028
  144.0 2.3 %copy-start = (bf16[896,1024]{1,0:T(8,128)(2,1)S(1)}, bf16[896,1024]{1,0:T(8,128)(2,1)}, u32[]{:S(2)}) copy-start(bf16[896,1024]{1,0:T(8,128)(2,1)} %get-tuple-element.18) | copy-start | bytes 5505028
  146.2 2.3 %copy-start.3 = (bf16[512,1024]{1,0:T(8,128)(2,1)S(1)}, bf16[512,1024]{1,0:T(8,128)(2,1)}, u32[]{:S(2)}) copy-start(bf16[512,1024]{1,0:T(8,128)(2,1)} %get-tuple-element.36) | copy-start | bytes 3145732
  148.5 1.6 %copy-start.2 = (bf16[512,1024]{1,0:T(8,128)(2,1)S(1)}, bf16[512,1024]{1,0:T(8,128)(2,1)}, u32[]{:S(2)}) copy-start(bf16[512,1024]{1,0:T(8,128)(2,1)} %get-tuple-element.37) | copy-start | bytes 3145732
